TPU v7x, 256 devices: a whole 4x4x8 slice. The times are simulated.
256 devices in a mesh: blk: 128 (over z, y, x), chan: 2 (over core).
Axes of the slice: x: 4, y: 4, z: 8, core: 2. Of those that a mesh axis runs over, the one named last changes fastest.
Arguments:
- inputs: bfloat16 [128, 512, 512], P('chan', 'blk'), may hold values from -6 to 6
- w_first: bfloat16 [3, 3, 128, 128], P(None, None, 'chan'), may hold values from -0.1875 to 0.1875
- w_second: bfloat16 [3, 3, 128, 128], P(None, None, 'chan'), may hold values from -0.1875 to 0.1875
- w_third: bfloat16 [3, 3, 256, 128], P(None, None, 'chan'), may hold values from -0.1875 to 0.1875
- cotangent: bfloat16 [256, 256, 256], P('chan', 'blk'), may hold values from -6 to 6
- mirror: int32 [128], P('blk'), may hold values from 0 to 1
Outputs:
- grad_inputs: bfloat16 [128, 512, 512], P('chan', 'blk')
- grad_first: float32 [3, 3, 128, 128], P(None, None, 'chan')
- grad_second: float32 [3, 3, 128, 128], P(None, None, 'chan')
- grad_third: float32 [3, 3, 256, 128], P(None, None, 'chan')
Inputs may be any that keep to these rules, and one draw needn't show every extreme that they name: `mirror`: 1 marks a tile whose columns are stored in reverse order, 0 a tile stored in the cycle's order.
All inputs are finite; a program needn't handle non-finite values.
Results may differ from a plain program's by a relative error of at most 0.024.
Values may be sent and summed in bfloat16 or wider, within the bound.
A program may use at most 64 MiB of HBM per device.

v0:
```python
import math

import jax
import jax.numpy as jnp
from jax import lax
from jax.sharding import PartitionSpec as P


def extended(shard, sides, width):
    for axis, dim in sides:
        devices, length = (lax.axis_size(axis), shard.shape[dim])
        up = [(i, (i + 1) % devices) for i in range(devices)]
        down = [(j, i) for i, j in up]
        last = lax.slice_in_dim(shard, length - width, length, axis=dim)
        leading = lax.slice_in_dim(shard, 0, width, axis=dim)
        before = lax.ppermute(last, axis, up)
        after = lax.ppermute(leading, axis, down)
        shard = jnp.concatenate([before, shard, after], axis=dim)
    return shard


def passed_along(shard, axis, by):
    devices = lax.axis_size(axis)
    return lax.ppermute(shard, axis, [(i, (i + by) % devices) for i in range(devices)])


def orient(block, mirrored):
    return jnp.where(mirrored == 1, block[..., ::-1], block)


def widen(active):
    gathered = lax.all_gather(active, "chan", axis=0, tiled=True)
    return extended(gathered, (("blk", 1),), 1)


def conv_taps(padded, weight):
    row_count = padded.shape[1] - 2
    col_count = padded.shape[2]
    framed = jnp.pad(padded, ((0, 0), (0, 0), (1, 1)))
    running = jnp.zeros((weight.shape[2], row_count, col_count), jnp.float32)
    for row_tap in range(3):
        for col_tap in range(3):
            running = running + jnp.einsum(
                "oi,irw->orw",
                weight[row_tap, col_tap],
                framed[:, row_tap : row_tap + row_count, col_tap : col_tap + col_count],
                preferred_element_type=jnp.float32,
            )
    return running


def weight_taps(grad_out, padded):
    row_count = grad_out.shape[1]
    col_count = grad_out.shape[2]
    framed = jnp.pad(padded, ((0, 0), (0, 0), (1, 1)))
    stacked = []
    for row_tap in range(3):
        line = []
        for col_tap in range(3):
            line.append(
                jnp.einsum(
                    "orw,irw->oi",
                    grad_out,
                    framed[:, row_tap : row_tap + row_count, col_tap : col_tap + col_count],
                    preferred_element_type=jnp.float32,
                )
            )
        stacked.append(jnp.stack(line))
    return jnp.stack(stacked)


def spread_taps(grad_out, weight):
    row_count = grad_out.shape[1]
    col_count = grad_out.shape[2]
    framed = jnp.pad(grad_out, ((0, 0), (2, 2), (2, 2)))
    running = jnp.zeros((weight.shape[3], row_count + 2, col_count), jnp.float32)
    for row_tap in range(3):
        for col_tap in range(3):
            row_start = 2 - row_tap
            col_start = 3 - col_tap
            running = running + jnp.einsum(
                "oi,orw->irw",
                weight[row_tap, col_tap],
                framed[:, row_start : row_start + row_count + 2, col_start : col_start + col_count],
                preferred_element_type=jnp.float32,
            )
    return running


def spread_stride(grad_out, weight):
    out_rows = grad_out.shape[1]
    out_cols = grad_out.shape[2]
    channels = weight.shape[3]
    framed = jnp.pad(grad_out, ((0, 0), (1, 1), (1, 1)))
    parity_rows = []
    for row_par in range(2):
        parity_cols = []
        for col_par in range(2):
            running = jnp.zeros((channels, out_rows + 1, out_cols + 1), jnp.float32)
            for row_tap in range(row_par, 3, 2):
                for col_tap in range(col_par, 3, 2):
                    row_start = 1 - row_tap // 2
                    col_start = 1 - col_tap // 2
                    running = running + jnp.einsum(
                        "oi,orw->irw",
                        weight[row_tap, col_tap],
                        framed[
                            :,
                            row_start : row_start + out_rows + 1,
                            col_start : col_start + out_cols + 1,
                        ],
                        preferred_element_type=jnp.float32,
                    )
            parity_cols.append(running)
        parity_rows.append(jnp.stack(parity_cols, axis=3))
    woven = jnp.stack(parity_rows, axis=2)
    woven = woven.reshape(channels, 2 * out_rows + 2, 2 * out_cols + 2)
    return woven[:, : 2 * out_rows + 1, 1 : 2 * out_cols + 1]


def fold_rims(grad_rows, both_sides):
    interior = grad_rows[:, 1:-1] if both_sides else grad_rows[:, 1:]
    from_next = passed_along(grad_rows[:, :1].astype(jnp.bfloat16), "blk", -1).astype(jnp.float32)
    if both_sides:
        from_prev = passed_along(grad_rows[:, -1:].astype(jnp.bfloat16), "blk", 1).astype(
            jnp.float32
        )
        return jnp.concatenate(
            [interior[:, :1] + from_prev, interior[:, 1:-1], interior[:, -1:] + from_next], axis=1
        )
    return jnp.concatenate([interior[:, :-1], interior[:, -1:] + from_next], axis=1)


def own_inputs(weight):
    whole = lax.all_gather(weight, "chan", axis=2, tiled=True)
    width = whole.shape[3] // lax.axis_size("chan")
    return lax.dynamic_slice_in_dim(whole, lax.axis_index("chan") * width, width, axis=3)


def input_grad(delta, weight):
    every = lax.all_gather(delta, "chan", axis=0, tiled=True)
    return fold_rims(spread_taps(every, weight), True)


def third_input_grad(upstream, weight):
    every = lax.all_gather(upstream, "chan", axis=0, tiled=True)
    return fold_rims(spread_stride(every, weight), False)


def parity_picker(cols, out_cols):
    source = lax.broadcasted_iota(jnp.int32, (cols, 3 * out_cols), 0)
    target = lax.broadcasted_iota(jnp.int32, (cols, 3 * out_cols), 1)
    wanted = 2 * (target % out_cols) + target // out_cols - 1
    return (source == wanted).astype(jnp.bfloat16)


def summed_over_cycle(parts, axis):
    devices = lax.axis_size(axis)
    flat = jnp.concatenate([p.reshape(-1) for p in parts])
    pieces = lax.all_to_all(flat.reshape(devices, -1), axis, 0, 0, tiled=True)
    total = jnp.sum(pieces, axis=0)
    spread = jnp.broadcast_to(total[None], (devices,) + total.shape)
    whole = lax.all_to_all(spread, axis, 0, 0, tiled=True).reshape(-1)
    out, start = [], 0
    for p in parts:
        out.append(whole[start : start + p.size].reshape(p.shape))
        start += p.size
    return out


def gelu_back(pre_act, grad_in):
    return jax.vjp(jax.nn.gelu, pre_act)[1](grad_in)[0]


def shards(inputs, w_first, w_second, w_third, cotangent, mirror):
    mirrored = mirror[0]
    oriented = orient(inputs, mirrored)
    upstream = orient(cotangent, mirrored)
    first_pad = widen(oriented)
    first_pre = conv_taps(first_pad, w_first)
    first_act = jax.nn.gelu(first_pre).astype(jnp.bfloat16)
    second_pad = widen(first_act)
    second_pre = conv_taps(second_pad, w_second)
    second_act = jax.nn.gelu(second_pre).astype(jnp.bfloat16)
    second_all = lax.all_gather(second_act, "chan", axis=0, tiled=True)
    wrap_top = passed_along(second_all[:, -1:], "blk", 1)
    stride_rows = jnp.concatenate([wrap_top, second_all], axis=1)
    out_rows = upstream.shape[1]
    out_cols = upstream.shape[2]
    by_parity = jnp.einsum(
        "irt,tk->irk",
        stride_rows,
        parity_picker(2 * out_cols, out_cols),
        preferred_element_type=jnp.float32,
    ).astype(jnp.bfloat16)
    spaced = jnp.stack([upstream, jnp.zeros_like(upstream)], axis=2).reshape(
        upstream.shape[0], 2 * out_rows, out_cols
    )
    row_placed = jnp.stack(
        [jnp.pad(spaced, ((0, 0), (row_tap, 1), (0, 0)))[:, : 2 * out_rows + 1] for row_tap in range(3)]
    )
    third_grad = jnp.stack(
        [
            jnp.einsum(
                "aosc,isc->aoi",
                row_placed,
                by_parity[:, :, col_tap * out_cols : (col_tap + 1) * out_cols],
                preferred_element_type=jnp.float32,
            )
            for col_tap in range(3)
        ],
        axis=1,
    )
    second_back = third_input_grad(upstream, own_inputs(w_third))
    second_delta = gelu_back(second_pre, second_back).astype(jnp.bfloat16)
    second_grad = weight_taps(second_delta, second_pad)
    first_back = input_grad(second_delta, own_inputs(w_second))
    first_delta = gelu_back(first_pre, first_back).astype(jnp.bfloat16)
    first_grad = weight_taps(first_delta, first_pad)
    input_back = input_grad(first_delta, own_inputs(w_first)).astype(jnp.bfloat16)
    reduced = summed_over_cycle((first_grad, second_grad, third_grad), "blk")
    cell_count = inputs.shape[1] * inputs.shape[2] * lax.axis_size("blk")
    return (
        orient(input_back, mirrored),
        reduced[0] / math.sqrt(cell_count),
        reduced[1] / math.sqrt(cell_count),
        reduced[2] / math.sqrt(cell_count // 4),
    )


def solution(mesh):
    placed = (
        P("chan", "blk", None),
        P(None, None, "chan", None),
        P(None, None, "chan", None),
        P(None, None, "chan", None),
        P("chan", "blk", None),
        P("blk"),
    )
    return jax.shard_map(
        shards,
        mesh=mesh,
        in_specs=placed,
        out_specs=(
            P("chan", "blk", None),
            P(None, None, "chan", None),
            P(None, None, "chan", None),
            P(None, None, "chan", None),
        ),
        check_vma=False,
    )
```

profile of v0, /device:TPU:8, one launch (start us, length us, event | category | flops | bytes accessed | tf_op | source)
XLA Modules:
  0.0 179.3 jit_solution(8476999491006758142)
XLA Ops:
  3.9 2.2 %all_gather.31 = bf16[128,4,512]{2,0,1:T(8,128)(2,1)S(1)} all-gather(bf16[64,4,512]{2,0,1:T(8,128)(2,1)S(1)} %broadcast_select_fusion.1), channel_id=1, replica_groups=mesh['blk'=128,'chan'=2] {'chan'}, dimensions={0}, use_global_device_ids=true | all-gather | bytes 786432 | tf_op jit(solution)/shard_map/all_gather | solution.py:32
  6.8 2.6 %collective-permute-start.2 = (bf16[128,1,512]{2,0,1:T(8,128)(2,1)}, bf16[128,1,512]{2,0,1:T(8,128)(2,1)}, u32[]{:S(2)}, u32[]{:S(2)}) collective-permute-start(bf16[128,1,512]{2,0,1:T(8,128)(2,1)} %get-tuple-element.35), channel_id=1, source_target_pairs={{2,0},{4,2},{6,4},{8,6},{10,8},{12,10},{14,12},{16,14},{18,16},{20... | collective-permute-start | bytes 393224 | tf_op jit(solution)/shard_map/ppermute | solution.py:17
  9.8 2.0 %all_gather.30 = bf16[256,2,256]{0,2,1:T(8,128)(2,1)S(1)} all-gather(bf16[128,2,256]{0,2,1:T(8,128)(2,1)S(1)} %broadcast_select_fusion.2), channel_id=1, replica_groups=mesh['blk'=128,'chan'=2] {'chan'}, dimensions={0}, use_global_device_ids=true | all-gather | bytes 393216 | tf_op jit(solution)/shard_map/all_gather | solution.py:146
  12.0 2.2 %all_gather.29 = bf16[3,3,256,128]{2,3,1,0:T(8,128)(2,1)S(1)} all-gather(bf16[3,3,128,128]{2,3,1,0:T(8,128)(2,1)S(1)} %copy.62), channel_id=1, replica_groups=mesh['blk'=128,'chan'=2] {'chan'}, dimensions={2}, use_global_device_ids=true | all-gather | bytes 884736 | tf_op jit(solution)/shard_map/all_gather | solution.py:135
  17.8 2.3 %reshape.57 = f32[64,6,514]{0,2,1:T(8,128)} reshape(f32[64,3,2,257,2]{0,4,3,2,1:T(2,128)S(1)} %copy.65) | data formatting | bytes 1579008 | tf_op jit(solution)/shard_map/reshape | solution.py:117
  21.1 4.2 %collective-permute-start = (bf16[64,1,512]{2,0,1:T(8,128)(2,1)S(1)}, bf16[64,1,512]{2,0,1:T(8,128)(2,1)}, u32[]{:S(2)}, u32[]{:S(2)}) collective-permute-start(bf16[64,1,512]{2,0,1:T(8,128)(2,1)S(1)} %copy.102), channel_id=1, source_target_pairs={{0,254},{2,0},{4,2},{6,4},{8,6},{10,8},{12,10},{14,12},{16,14},{18... | collective-permute-start | bytes 196616 | tf_op jit(solution)/shard_map/ppermute | solution.py:24
  28.0 2.0 %all_gather.28 = bf16[3,3,128,128]{3,2,1,0:T(8,128)(2,1)S(1)} all-gather(bf16[3,3,64,128]{3,2,1,0:T(8,128)(2,1)S(1)} %copy-done.1), channel_id=1, replica_groups=mesh['blk'=128,'chan'=2] {'chan'}, dimensions={2}, use_global_device_ids=true | all-gather | bytes 442368 | tf_op jit(solution)/shard_map/all_gather | solution.py:135
  35.2 2.2 %all_gather.32 = bf16[128,4,512]{2,0,1:T(8,128)(2,1)S(1)} all-gather(bf16[64,4,512]{2,0,1:T(8,128)(2,1)S(1)} %get-tuple-element.43), channel_id=1, replica_groups=mesh['blk'=128,'chan'=2] {'chan'}, dimensions={0}, use_global_device_ids=true | all-gather | bytes 786432 | tf_op jit(solution)/shard_map/all_gather | solution.py:32
  37.5 2.0 %collective-permute-start.3 = (bf16[128,1,512]{2,0,1:T(8,128)(2,1)S(1)}, bf16[128,1,512]{2,0,1:T(8,128)(2,1)S(1)}, u32[]{:S(2)}, u32[]{:S(2)}) collective-permute-start(bf16[128,1,512]{2,0,1:T(8,128)(2,1)S(1)} %get-tuple-element.32), channel_id=1, source_target_pairs={{0,2},{2,4},{4,6},{6,8},{8,10},{10,12},{12,14},{14,16},{16,18},{18... | collective-permute-start | bytes 393224 | tf_op jit(solution)/shard_map/ppermute | solution.py:16
  40.3 2.7 %collective-permute-done.4 = bf16[128,1,512]{2,0,1:T(8,128)(2,1)S(1)} collective-permute-done((bf16[128,1,512]{2,0,1:T(8,128)(2,1)S(1)}, bf16[128,1,512]{2,0,1:T(8,128)(2,1)S(1)}, u32[]{:S(2)}, u32[]{:S(2)}) %collective-permute-start.4) | collective-permute-done | bytes 131104 | tf_op jit(solution)/shard_map/ppermute | solution.py:17
  43.0 2.4 %collective-permute-done.3 = bf16[128,1,512]{2,0,1:T(8,128)(2,1)S(1)} collective-permute-done((bf16[128,1,512]{2,0,1:T(8,128)(2,1)S(1)}, bf16[128,1,512]{2,0,1:T(8,128)(2,1)S(1)}, u32[]{:S(2)}, u32[]{:S(2)}) %collective-permute-start.3) | collective-permute-done | bytes 131104 | tf_op jit(solution)/shard_map/ppermute | solution.py:16
  48.6 2.2 %all_gather.33 = bf16[128,4,512]{2,0,1:T(8,128)(2,1)S(1)} all-gather(bf16[64,4,512]{2,0,1:T(8,128)(2,1)S(1)} %get-tuple-element.31), channel_id=1, replica_groups=mesh['blk'=128,'chan'=2] {'chan'}, dimensions={0}, use_global_device_ids=true | all-gather | bytes 786432 | tf_op jit(solution)/shard_map/all_gather | solution.py:141
  56.9 4.1 %collective-permute-start.6 = (bf16[64,1,512]{2,0,1:T(8,128)(2,1)S(1)}, bf16[64,1,512]{2,0,1:T(8,128)(2,1)S(1)}, u32[]{:S(2)}, u32[]{:S(2)}) collective-permute-start(bf16[64,1,512]{2,0,1:T(8,128)(2,1)S(1)} %get-tuple-element.39), channel_id=1, source_target_pairs={{0,254},{2,0},{4,2},{6,4},{8,6},{10,8},{12,10},{14,12},{16,14},{18... | collective-permute-start | bytes 196616 | tf_op jit(solution)/shard_map/ppermute | solution.py:24
  61.1 2.2 %all_gather.35 = bf16[128,4,512]{2,0,1:T(8,128)(2,1)S(1)} all-gather(bf16[64,4,512]{2,0,1:T(8,128)(2,1)S(1)} %get-tuple-element.30), channel_id=1, replica_groups=mesh['blk'=128,'chan'=2] {'chan'}, dimensions={0}, use_global_device_ids=true | all-gather | bytes 786432 | tf_op jit(solution)/shard_map/all_gather | solution.py:185
  68.6 6.0 %collective-permute-done.9 = bf16[128,1,512]{2,0,1:T(8,128)(2,1)S(1)} collective-permute-done((bf16[128,1,512]{2,0,1:T(8,128)(2,1)S(1)}, bf16[128,1,512]{2,0,1:T(8,128)(2,1)S(1)}, u32[]{:S(2)}, u32[]{:S(2)}) %collective-permute-start.9) | collective-permute-done | bytes 131104 | tf_op jit(solution)/shard_map/ppermute | solution.py:24
  77.9 23.4 %all-to-all-start = ((f32[128,1,2304]{2,1,0:T(1,128)}), f32[128,1,2304]{2,1,0:T(1,128)S(1)}, u32[]{:S(2)}, u32[]{:S(2)}) async-start(f32[128,1,2304]{2,1,0:T(1,128)} %bitcast.162), calls=%async_computation | async-start | bytes 2359296 | tf_op jit(solution)/shard_map/all_to_all | solution.py:160
  101.3 2.0 %all_gather.27 = bf16[3,3,128,128]{3,2,1,0:T(8,128)(2,1)S(1)} all-gather(bf16[3,3,64,128]{3,2,1,0:T(8,128)(2,1)S(1)} %copy-done), channel_id=1, replica_groups=mesh['blk'=128,'chan'=2] {'chan'}, dimensions={2}, use_global_device_ids=true | all-gather | bytes 442368 | tf_op jit(solution)/shard_map/all_gather | solution.py:135
  103.3 2.2 %all_gather.34 = bf16[128,4,512]{2,0,1:T(8,128)(2,1)S(1)} all-gather(bf16[64,4,512]{2,0,1:T(8,128)(2,1)S(1)} %fusion.38), channel_id=1, replica_groups=mesh['blk'=128,'chan'=2] {'chan'}, dimensions={0}, use_global_device_ids=true | all-gather | bytes 786432 | tf_op jit(solution)/shard_map/all_gather | solution.py:141
  106.6 27.9 %all-to-all-done = f32[128,1,2304]{2,1,0:T(1,128)S(1)} async-done(((f32[128,1,2304]{2,1,0:T(1,128)}), f32[128,1,2304]{2,1,0:T(1,128)S(1)}, u32[]{:S(2)}, u32[]{:S(2)}) %all-to-all-start) | async-done | bytes 1179680 | tf_op jit(solution)/shard_map/all_to_all | solution.py:160
  136.9 6.6 %all-to-all-start.1 = ((f32[128,1,2304]{2,1,0:T(1,128)}), f32[128,1,2304]{2,1,0:T(1,128)S(1)}, u32[]{:S(2)}, u32[]{:S(2)}) async-start(f32[128,1,2304]{2,1,0:T(1,128)} %broadcast_in_dim.2), calls=%async_computation.1 | async-start | bytes 2359296 | tf_op jit(solution)/shard_map/all_to_all | solution.py:163
  145.9 1.8 %collective-permute-start.7 = (bf16[64,1,512]{2,0,1:T(8,128)(2,1)S(1)}, bf16[64,1,512]{2,0,1:T(8,128)(2,1)S(1)}, u32[]{:S(2)}, u32[]{:S(2)}) collective-permute-start(bf16[64,1,512]{2,0,1:T(8,128)(2,1)S(1)} %get-tuple-element.36), channel_id=1, source_target_pairs={{0,2},{2,4},{4,6},{6,8},{8,10},{10,12},{12,14},{14,16},{16,18},{18... | collective-permute-start | bytes 196616 | tf_op jit(solution)/shard_map/ppermute | solution.py:24
  147.7 2.7 %collective-permute-start.8 = (bf16[64,1,512]{2,0,1:T(8,128)(2,1)S(1)}, bf16[64,1,512]{2,0,1:T(8,128)(2,1)S(1)}, u32[]{:S(2)}, u32[]{:S(2)}) collective-permute-start(bf16[64,1,512]{2,0,1:T(8,128)(2,1)S(1)} %get-tuple-element.37), channel_id=1, source_target_pairs={{0,254},{2,0},{4,2},{6,4},{8,6},{10,8},{12,10},{14,12},{16,14},{18... | collective-permute-start | bytes 196616 | tf_op jit(solution)/shard_map/ppermute | solution.py:24
  150.4 3.4 %collective-permute-done.7 = bf16[64,1,512]{2,0,1:T(8,128)(2,1)S(1)} collective-permute-done((bf16[64,1,512]{2,0,1:T(8,128)(2,1)S(1)}, bf16[64,1,512]{2,0,1:T(8,128)(2,1)S(1)}, u32[]{:S(2)}, u32[]{:S(2)}) %collective-permute-start.7) | collective-permute-done | bytes 65568 | tf_op jit(solution)/shard_map/ppermute | solution.py:24
  155.3 21.2 %all-to-all-done.1 = f32[128,1,2304]{2,1,0:T(1,128)S(1)} async-done(((f32[128,1,2304]{2,1,0:T(1,128)}), f32[128,1,2304]{2,1,0:T(1,128)S(1)}, u32[]{:S(2)}, u32[]{:S(2)}) %all-to-all-start.1) | async-done | bytes 1179680 | tf_op jit(solution)/shard_map/all_to_all | solution.py:163
  (139 shorter events, 44.7 us)
Async XLA Ops:
  0.6 8.8 %copy-start.3 = (bf16[128,2,256]{2,1,0:T(2,128)(2,1)S(1)}, bf16[128,2,256]{2,1,0:T(2,128)(2,1)}, u32[]{:S(2)}) copy-start(bf16[128,2,256]{2,1,0:T(2,128)(2,1)} %param.10) | copy-start | bytes 393220
  2.8 9.0 %copy-start.2 = (bf16[3,3,128,128]{3,2,1,0:T(8,128)(2,1)S(1)}, bf16[3,3,128,128]{3,2,1,0:T(8,128)(2,1)}, u32[]{:S(2)}) copy-start(bf16[3,3,128,128]{3,2,1,0:T(8,128)(2,1)} %param.9) | copy-start | bytes 884740
  6.8 23.4 %collective-permute-start.2 = (bf16[128,1,512]{2,0,1:T(8,128)(2,1)}, bf16[128,1,512]{2,0,1:T(8,128)(2,1)}, u32[]{:S(2)}, u32[]{:S(2)}) collective-permute-start(bf16[128,1,512]{2,0,1:T(8,128)(2,1)} %get-tuple-element.35), channel_id=1, source_target_pairs={{2,0},{4,2},{6,4},{8,6},{10,8},{12,10},{14,12},{16,14},{18,16},{20... | collective-permute-start | bytes 393224 | tf_op jit(solution)/shard_map/ppermute | solution.py:17
  9.4 20.8 %collective-permute-start.1 = (bf16[128,1,512]{2,0,1:T(8,128)(2,1)}, bf16[128,1,512]{2,0,1:T(8,128)(2,1)S(1)}, u32[]{:S(2)}, u32[]{:S(2)}) collective-permute-start(bf16[128,1,512]{2,0,1:T(8,128)(2,1)} %get-tuple-element.34), channel_id=1, source_target_pairs={{0,2},{2,4},{4,6},{6,8},{8,10},{10,12},{12,14},{14,16},{16,18},{18... | collective-permute-start | bytes 393224 | tf_op jit(solution)/shard_map/ppermute | solution.py:16
  21.1 18.4 %collective-permute-start = (bf16[64,1,512]{2,0,1:T(8,128)(2,1)S(1)}, bf16[64,1,512]{2,0,1:T(8,128)(2,1)}, u32[]{:S(2)}, u32[]{:S(2)}) collective-permute-start(bf16[64,1,512]{2,0,1:T(8,128)(2,1)S(1)} %copy.102), channel_id=1, source_target_pairs={{0,254},{2,0},{4,2},{6,4},{8,6},{10,8},{12,10},{14,12},{16,14},{18... | collective-permute-start | bytes 196616 | tf_op jit(solution)/shard_map/ppermute | solution.py:24
  26.3 1.7 copy-start.1
  30.1 1.5 copy-start
  37.4 5.6 %collective-permute-start.4 = (bf16[128,1,512]{2,0,1:T(8,128)(2,1)S(1)}, bf16[128,1,512]{2,0,1:T(8,128)(2,1)S(1)}, u32[]{:S(2)}, u32[]{:S(2)}) collective-permute-start(bf16[128,1,512]{2,0,1:T(8,128)(2,1)S(1)} %get-tuple-element.33), channel_id=1, source_target_pairs={{2,0},{4,2},{6,4},{8,6},{10,8},{12,10},{14,12},{16,14},{18,16},{20... | collective-permute-start | bytes 393224 | tf_op jit(solution)/shard_map/ppermute | solution.py:17
  37.5 7.9 %collective-permute-start.3 = (bf16[128,1,512]{2,0,1:T(8,128)(2,1)S(1)}, bf16[128,1,512]{2,0,1:T(8,128)(2,1)S(1)}, u32[]{:S(2)}, u32[]{:S(2)}) collective-permute-start(bf16[128,1,512]{2,0,1:T(8,128)(2,1)S(1)} %get-tuple-element.32), channel_id=1, source_target_pairs={{0,2},{2,4},{4,6},{6,8},{8,10},{10,12},{12,14},{14,16},{16,18},{18... | collective-permute-start | bytes 393224 | tf_op jit(solution)/shard_map/ppermute | solution.py:16
  56.8 7.4 %collective-permute-start.5 = (bf16[64,1,512]{2,0,1:T(8,128)(2,1)S(1)}, bf16[64,1,512]{2,0,1:T(8,128)(2,1)S(1)}, u32[]{:S(2)}, u32[]{:S(2)}) collective-permute-start(bf16[64,1,512]{2,0,1:T(8,128)(2,1)S(1)} %get-tuple-element.38), channel_id=1, source_target_pairs={{0,2},{2,4},{4,6},{6,8},{8,10},{10,12},{12,14},{14,16},{16,18},{18... | collective-permute-start | bytes 196616 | tf_op jit(solution)/shard_map/ppermute | solution.py:24
  56.9 7.3 %collective-permute-start.6 = (bf16[64,1,512]{2,0,1:T(8,128)(2,1)S(1)}, bf16[64,1,512]{2,0,1:T(8,128)(2,1)S(1)}, u32[]{:S(2)}, u32[]{:S(2)}) collective-permute-start(bf16[64,1,512]{2,0,1:T(8,128)(2,1)S(1)} %get-tuple-element.39), channel_id=1, source_target_pairs={{0,254},{2,0},{4,2},{6,4},{8,6},{10,8},{12,10},{14,12},{16,14},{18... | collective-permute-start | bytes 196616 | tf_op jit(solution)/shard_map/ppermute | solution.py:24
  63.3 11.4 %collective-permute-start.9 = (bf16[128,1,512]{2,0,1:T(8,128)(2,1)S(1)}, bf16[128,1,512]{2,0,1:T(8,128)(2,1)S(1)}, u32[]{:S(2)}, u32[]{:S(2)}) collective-permute-start(bf16[128,1,512]{2,0,1:T(8,128)(2,1)S(1)} %slice.526), channel_id=1, source_target_pairs={{0,2},{2,4},{4,6},{6,8},{8,10},{10,12},{12,14},{14,16},{16,18},{18... | collective-permute-start | bytes 393224 | tf_op jit(solution)/shard_map/ppermute | solution.py:24
  77.9 56.7 %all-to-all-start = ((f32[128,1,2304]{2,1,0:T(1,128)}), f32[128,1,2304]{2,1,0:T(1,128)S(1)}, u32[]{:S(2)}, u32[]{:S(2)}) async-start(f32[128,1,2304]{2,1,0:T(1,128)} %bitcast.162), calls=%async_computation | async-start | bytes 2359296 | tf_op jit(solution)/shard_map/all_to_all | solution.py:160
  136.9 39.7 %all-to-all-start.1 = ((f32[128,1,2304]{2,1,0:T(1,128)}), f32[128,1,2304]{2,1,0:T(1,128)S(1)}, u32[]{:S(2)}, u32[]{:S(2)}) async-start(f32[128,1,2304]{2,1,0:T(1,128)} %broadcast_in_dim.2), calls=%async_computation.1 | async-start | bytes 2359296 | tf_op jit(solution)/shard_map/all_to_all | solution.py:163
  145.9 7.9 %collective-permute-start.7 = (bf16[64,1,512]{2,0,1:T(8,128)(2,1)S(1)}, bf16[64,1,512]{2,0,1:T(8,128)(2,1)S(1)}, u32[]{:S(2)}, u32[]{:S(2)}) collective-permute-start(bf16[64,1,512]{2,0,1:T(8,128)(2,1)S(1)} %get-tuple-element.36), channel_id=1, source_target_pairs={{0,2},{2,4},{4,6},{6,8},{8,10},{10,12},{12,14},{14,16},{16,18},{18... | collective-permute-start | bytes 196616 | tf_op jit(solution)/shard_map/ppermute | solution.py:24
  147.7 6.1 %collective-permute-start.8 = (bf16[64,1,512]{2,0,1:T(8,128)(2,1)S(1)}, bf16[64,1,512]{2,0,1:T(8,128)(2,1)S(1)}, u32[]{:S(2)}, u32[]{:S(2)}) collective-permute-start(bf16[64,1,512]{2,0,1:T(8,128)(2,1)S(1)} %get-tuple-element.37), channel_id=1, source_target_pairs={{0,254},{2,0},{4,2},{6,4},{8,6},{10,8},{12,10},{14,12},{16,14},{18... | collective-permute-start | bytes 196616 | tf_op jit(solution)/shard_map/ppermute | solution.py:24
where the time goes:
time: 180 us; the launch traced here: 179 us
  waiting for transfers between devices  63.6 us (35%)
  starting transfers between devices  47.9 us (27%)
  matrix products  24.2 us (13%)
  blocking collectives  19.2 us (11%)
  local copies, waits for them, and re-layouts  13.2 us (7%)
  other arithmetic  9.17 us (5%)
  between operations  2.13 us (1%)
    all_to_all x1, waiting for transfers between devices, summed_over_cycle(): pieces = lax.all_to_all(flat.reshape(devices, -1), axis, 0, 0, tiled=True)  27.9 us
    all_to_all x1, starting transfers between devices, summed_over_cycle(): pieces = lax.all_to_all(flat.reshape(devices, -1), axis, 0, 0, tiled=True)  23.4 us
    all_to_all x1, waiting for transfers between devices, summed_over_cycle(): whole = lax.all_to_all(spread, axis, 0, 0, tiled=True).reshape(-1)  21.2 us
    ppermute x6, starting transfers between devices, passed_along(): lax.ppermute(shard, axis, [(i, (i + by) % devices) for i in range(devices)])  13.2 us
    ppermute x6, waiting for transfers between devices, passed_along(): lax.ppermute(shard, axis, [(i, (i + by) % devices) for i in range(devices)])  9.43 us
    dot_general x18, matrix products, spread_taps(): jnp.einsum('oi,orw->irw', weight[row_tap, col_tap], framed[:, row_start:r...  7.12 us
    dot_general x18, matrix products, weight_taps(): jnp.einsum('orw,irw->oi', grad_out, framed[:, row_tap:row_tap + row_count...  6.73 us
    all_to_all x1, starting transfers between devices, summed_over_cycle(): whole = lax.all_to_all(spread, axis, 0, 0, tiled=True).reshape(-1)  6.59 us
  transfers between devices with their start and end apart: 12, of which 6 were waited for; matrix products, arithmetic and copies ran while one was open for 14% of the time, Pallas kernels for 0%

commit v1 on v0

--- a/solution.py
+++ b/solution.py
@@ -218,7 +218,8 @@
     first_delta = gelu_back(first_pre, first_back).astype(jnp.bfloat16)
     first_grad = weight_taps(first_delta, first_pad)
     input_back = input_grad(first_delta, own_inputs(w_first)).astype(jnp.bfloat16)
-    reduced = summed_over_cycle((first_grad, second_grad, third_grad), "blk")
+    input_back, grads = lax.optimization_barrier((input_back, (first_grad, second_grad, third_grad)))
+    reduced = summed_over_cycle(grads, "blk")
     cell_count = inputs.shape[1] * inputs.shape[2] * lax.axis_size("blk")
     return (
         orient(input_back, mirrored),

time: 180 us -> 192 us (1.067)
  blocking collectives: 19.2 us -> 79.1 us
  waiting for transfers between devices: 63.6 us -> 36.1 us
  starting transfers between devices: 47.9 us -> 27.1 us
    all_to_all x0 -> x1, blocking collectives: none -> 59.8 us  [summed_over_cycle(): pieces = lax.all_to_all(flat.reshape(devices, -1), axis, 0, 0, tiled=True)]
    all_to_all x1 -> x0, waiting for transfers between devices: 27.9 us -> none  [summed_over_cycle(): pieces = lax.all_to_all(flat.reshape(devices, -1), axis, 0, 0, tiled=True)]
    all_to_all x1 -> x0, starting transfers between devices: 23.4 us -> none  [summed_over_cycle(): pieces = lax.all_to_all(flat.reshape(devices, -1), axis, 0, 0, tiled=True)]
    all_to_all x1, waiting for transfers between devices: 21.2 us -> 31.1 us  [summed_over_cycle(): whole = lax.all_to_all(spread, axis, 0, 0, tiled=True).reshape(-1)]
    ppermute x6, waiting for transfers between devices: 9.43 us -> 0.02 us  [passed_along(): lax.ppermute(shard, axis, [(i, (i + by) % devices) for i in range(devices)])]
    ppermute x6, starting transfers between devices: 13.2 us -> 15.8 us  [passed_along(): lax.ppermute(shard, axis, [(i, (i + by) % devices) for i in range(devices)])]
  transfers between devices with their start and end apart: 12 -> 11, of which waited for: 6 -> 3; matrix products, arithmetic and copies ran while one was open for 14% -> 15% of each run, Pallas kernels for 0% -> 0%
where the time goes in v1:
time: 192 us
  blocking collectives  79.1 us (41%)
  waiting for transfers between devices  36.1 us (19%)
  starting transfers between devices  27.1 us (14%)
  matrix products  24.2 us (13%)
  local copies, waits for them, and re-layouts  13.8 us (7%)
  other arithmetic  9.32 us (5%)
  between operations  2.21 us (1%)
    all_to_all x1, blocking collectives, summed_over_cycle(): pieces = lax.all_to_all(flat.reshape(devices, -1), axis, 0, 0, tiled=True)  59.8 us
    all_to_all x1, waiting for transfers between devices, summed_over_cycle(): whole = lax.all_to_all(spread, axis, 0, 0, tiled=True).reshape(-1)  31.1 us
    ppermute x6, starting transfers between devices, passed_along(): lax.ppermute(shard, axis, [(i, (i + by) % devices) for i in range(devices)])  15.8 us
    dot_general x18, matrix products, spread_taps(): jnp.einsum('oi,orw->irw', weight[row_tap, col_tap], framed[:, row_start:r...  7.12 us
    dot_general x18, matrix products, weight_taps(): jnp.einsum('orw,irw->oi', grad_out, framed[:, row_tap:row_tap + row_count...  6.73 us
    all_to_all x1, starting transfers between devices, summed_over_cycle(): whole = lax.all_to_all(spread, axis, 0, 0, tiled=True).reshape(-1)  6.52 us
    all_gather x3, blocking collectives, own_inputs(): whole = lax.all_gather(weight, 'chan', axis=2, tiled=True)  6.25 us
    dot_general x18, matrix products, conv_taps(): jnp.einsum('oi,irw->orw', weight[row_tap, col_tap], framed[:, row_tap:row...  6.14 us
  transfers between devices with their start and end apart: 11, of which 3 were waited for; matrix products, arithmetic and copies ran while one was open for 15% of the time, Pallas kernels for 0%

profile of v1, /device:TPU:8, one launch (start us, length us, event | category | flops | bytes accessed | tf_op | source)
XLA Modules:
  0.0 191.9 jit_solution(4310463290330476869)
XLA Ops:
  3.9 2.2 %all_gather.31 = bf16[128,4,512]{2,0,1:T(8,128)(2,1)S(1)} all-gather(bf16[64,4,512]{2,0,1:T(8,128)(2,1)S(1)} %broadcast_select_fusion.1), channel_id=1, replica_groups=mesh['blk'=128,'chan'=2] {'chan'}, dimensions={0}, use_global_device_ids=true | all-gather | bytes 786432 | tf_op jit(solution)/shard_map/all_gather | solution.py:32
  6.8 2.6 %collective-permute-start.2 = (bf16[128,1,512]{2,0,1:T(8,128)(2,1)}, bf16[128,1,512]{2,0,1:T(8,128)(2,1)}, u32[]{:S(2)}, u32[]{:S(2)}) collective-permute-start(bf16[128,1,512]{2,0,1:T(8,128)(2,1)} %get-tuple-element.43), channel_id=1, source_target_pairs={{2,0},{4,2},{6,4},{8,6},{10,8},{12,10},{14,12},{16,14},{18,16},{20... | collective-permute-start | bytes 393224 | tf_op jit(solution)/shard_map/ppermute | solution.py:17
  9.8 2.0 %all_gather.30 = bf16[256,2,256]{0,2,1:T(8,128)(2,1)S(1)} all-gather(bf16[128,2,256]{0,2,1:T(8,128)(2,1)S(1)} %broadcast_select_fusion.2), channel_id=1, replica_groups=mesh['blk'=128,'chan'=2] {'chan'}, dimensions={0}, use_global_device_ids=true | all-gather | bytes 393216 | tf_op jit(solution)/shard_map/all_gather | solution.py:146
  12.0 2.2 %all_gather.29 = bf16[3,3,256,128]{2,3,1,0:T(8,128)(2,1)S(1)} all-gather(bf16[3,3,128,128]{2,3,1,0:T(8,128)(2,1)S(1)} %copy.62), channel_id=1, replica_groups=mesh['blk'=128,'chan'=2] {'chan'}, dimensions={2}, use_global_device_ids=true | all-gather | bytes 884736 | tf_op jit(solution)/shard_map/all_gather | solution.py:135
  17.8 2.3 %reshape.57 = f32[64,6,514]{0,2,1:T(8,128)} reshape(f32[64,3,2,257,2]{0,4,3,2,1:T(2,128)S(1)} %copy.65) | data formatting | bytes 1579008 | tf_op jit(solution)/shard_map/reshape | solution.py:117
  21.7 4.1 %collective-permute-start = (bf16[64,1,512]{2,0,1:T(8,128)(2,1)}, bf16[64,1,512]{2,0,1:T(8,128)(2,1)}, u32[]{:S(2)}, u32[]{:S(2)}) collective-permute-start(bf16[64,1,512]{2,0,1:T(8,128)(2,1)} %copy.102), channel_id=1, source_target_pairs={{0,254},{2,0},{4,2},{6,4},{8,6},{10,8},{12,10},{14,12},{16,14},{18... | collective-permute-start | bytes 196616 | tf_op jit(solution)/shard_map/ppermute | solution.py:24
  29.7 2.0 %all_gather.28 = bf16[3,3,128,128]{3,2,1,0:T(8,128)(2,1)S(1)} all-gather(bf16[3,3,64,128]{3,2,1,0:T(8,128)(2,1)S(1)} %copy-done.1), channel_id=1, replica_groups=mesh['blk'=128,'chan'=2] {'chan'}, dimensions={2}, use_global_device_ids=true | all-gather | bytes 442368 | tf_op jit(solution)/shard_map/all_gather | solution.py:135
  31.7 2.0 %all_gather.27 = bf16[3,3,128,128]{3,2,1,0:T(8,128)(2,1)S(1)} all-gather(bf16[3,3,64,128]{3,2,1,0:T(8,128)(2,1)S(1)} %copy-done), channel_id=1, replica_groups=mesh['blk'=128,'chan'=2] {'chan'}, dimensions={2}, use_global_device_ids=true | all-gather | bytes 442368 | tf_op jit(solution)/shard_map/all_gather | solution.py:135
  34.0 1.4 fusion.18
  38.9 2.2 %all_gather.32 = bf16[128,4,512]{2,0,1:T(8,128)(2,1)S(1)} all-gather(bf16[64,4,512]{2,0,1:T(8,128)(2,1)S(1)} %get-tuple-element.51), channel_id=1, replica_groups=mesh['blk'=128,'chan'=2] {'chan'}, dimensions={0}, use_global_device_ids=true | all-gather | bytes 786432 | tf_op jit(solution)/shard_map/all_gather | solution.py:32
  41.2 2.0 %collective-permute-start.3 = (bf16[128,1,512]{2,0,1:T(8,128)(2,1)S(1)}, bf16[128,1,512]{2,0,1:T(8,128)(2,1)S(1)}, u32[]{:S(2)}, u32[]{:S(2)}) collective-permute-start(bf16[128,1,512]{2,0,1:T(8,128)(2,1)S(1)} %get-tuple-element.40), channel_id=1, source_target_pairs={{0,2},{2,4},{4,6},{6,8},{8,10},{10,12},{12,14},{14,16},{16,18},{18... | collective-permute-start | bytes 393224 | tf_op jit(solution)/shard_map/ppermute | solution.py:16
  44.0 2.7 %collective-permute-done.4 = bf16[128,1,512]{2,0,1:T(8,128)(2,1)S(1)} collective-permute-done((bf16[128,1,512]{2,0,1:T(8,128)(2,1)S(1)}, bf16[128,1,512]{2,0,1:T(8,128)(2,1)S(1)}, u32[]{:S(2)}, u32[]{:S(2)}) %collective-permute-start.4) | collective-permute-done | bytes 131104 | tf_op jit(solution)/shard_map/ppermute | solution.py:17
  46.7 2.4 %collective-permute-done.3 = bf16[128,1,512]{2,0,1:T(8,128)(2,1)S(1)} collective-permute-done((bf16[128,1,512]{2,0,1:T(8,128)(2,1)S(1)}, bf16[128,1,512]{2,0,1:T(8,128)(2,1)S(1)}, u32[]{:S(2)}, u32[]{:S(2)}) %collective-permute-start.3) | collective-permute-done | bytes 131104 | tf_op jit(solution)/shard_map/ppermute | solution.py:16
  52.3 2.2 %all_gather.33 = bf16[128,4,512]{2,0,1:T(8,128)(2,1)S(1)} all-gather(bf16[64,4,512]{2,0,1:T(8,128)(2,1)S(1)} %get-tuple-element.39), channel_id=1, replica_groups=mesh['blk'=128,'chan'=2] {'chan'}, dimensions={0}, use_global_device_ids=true | all-gather | bytes 786432 | tf_op jit(solution)/shard_map/all_gather | solution.py:141
  60.6 4.1 %collective-permute-start.6 = (bf16[64,1,512]{2,0,1:T(8,128)(2,1)S(1)}, bf16[64,1,512]{2,0,1:T(8,128)(2,1)S(1)}, u32[]{:S(2)}, u32[]{:S(2)}) collective-permute-start(bf16[64,1,512]{2,0,1:T(8,128)(2,1)S(1)} %get-tuple-element.47), channel_id=1, source_target_pairs={{0,254},{2,0},{4,2},{6,4},{8,6},{10,8},{12,10},{14,12},{16,14},{18... | collective-permute-start | bytes 196616 | tf_op jit(solution)/shard_map/ppermute | solution.py:24
  64.8 2.2 %all_gather.35 = bf16[128,4,512]{2,0,1:T(8,128)(2,1)S(1)} all-gather(bf16[64,4,512]{2,0,1:T(8,128)(2,1)S(1)} %get-tuple-element.38), channel_id=1, replica_groups=mesh['blk'=128,'chan'=2] {'chan'}, dimensions={0}, use_global_device_ids=true | all-gather | bytes 786432 | tf_op jit(solution)/shard_map/all_gather | solution.py:185
  68.2 2.4 %all_gather.34 = bf16[128,4,512]{2,0,1:T(8,128)(2,1)S(1)} all-gather(bf16[64,4,512]{2,0,1:T(8,128)(2,1)S(1)} %fusion.38), channel_id=1, replica_groups=mesh['blk'=128,'chan'=2] {'chan'}, dimensions={0}, use_global_device_ids=true | all-gather | bytes 786432 | tf_op jit(solution)/shard_map/all_gather | solution.py:141
  76.7 7.3 %collective-permute-start.8 = (bf16[64,1,512]{2,0,1:T(8,128)(2,1)S(1)}, bf16[64,1,512]{2,0,1:T(8,128)(2,1)S(1)}, u32[]{:S(2)}, u32[]{:S(2)}) collective-permute-start(bf16[64,1,512]{2,0,1:T(8,128)(2,1)S(1)} %get-tuple-element.45), channel_id=1, source_target_pairs={{0,254},{2,0},{4,2},{6,4},{8,6},{10,8},{12,10},{14,12},{16,14},{18... | collective-permute-start | bytes 196616 | tf_op jit(solution)/shard_map/ppermute | solution.py:24
  88.0 59.8 %all_to_all.15 = f32[128,1,2304]{2,1,0:T(1,128)S(1)} all-to-all(f32[128,1,2304]{2,1,0:T(1,128)S(1)} %bitcast.399), channel_id=1, replica_groups=mesh['blk'=128,'chan'=2] {'blk'}, dimensions={0} | all-to-all | bytes 2359296 | tf_op jit(solution)/shard_map/all_to_all | solution.py:160
  148.5 1.6 broadcast_in_dim.2
  150.1 6.5 %all-to-all-start.1 = ((f32[128,1,2304]{2,1,0:T(1,128)}), f32[128,1,2304]{2,1,0:T(1,128)S(1)}, u32[]{:S(2)}, u32[]{:S(2)}) async-start(f32[128,1,2304]{2,1,0:T(1,128)} %broadcast_in_dim.2), calls=%async_computation.1 | async-start | bytes 2359296 | tf_op jit(solution)/shard_map/all_to_all | solution.py:163
  158.1 31.1 %all-to-all-done.1 = f32[128,1,2304]{2,1,0:T(1,128)S(1)} async-done(((f32[128,1,2304]{2,1,0:T(1,128)}), f32[128,1,2304]{2,1,0:T(1,128)S(1)}, u32[]{:S(2)}, u32[]{:S(2)}) %all-to-all-start.1) | async-done | bytes 1179680 | tf_op jit(solution)/shard_map/all_to_all | solution.py:163
  189.1 1.4 slice_multiply_fusion.1
  190.6 1.3 slice_multiply_fusion
  (146 shorter events, 39.6 us)
Async XLA Ops:
  0.6 8.8 %copy-start.3 = (bf16[128,2,256]{2,1,0:T(2,128)(2,1)S(1)}, bf16[128,2,256]{2,1,0:T(2,128)(2,1)}, u32[]{:S(2)}) copy-start(bf16[128,2,256]{2,1,0:T(2,128)(2,1)} %param.10) | copy-start | bytes 393220
  2.8 9.0 %copy-start.2 = (bf16[3,3,128,128]{3,2,1,0:T(8,128)(2,1)S(1)}, bf16[3,3,128,128]{3,2,1,0:T(8,128)(2,1)}, u32[]{:S(2)}) copy-start(bf16[3,3,128,128]{3,2,1,0:T(8,128)(2,1)} %param.9) | copy-start | bytes 884740
  6.8 27.1 %collective-permute-start.2 = (bf16[128,1,512]{2,0,1:T(8,128)(2,1)}, bf16[128,1,512]{2,0,1:T(8,128)(2,1)}, u32[]{:S(2)}, u32[]{:S(2)}) collective-permute-start(bf16[128,1,512]{2,0,1:T(8,128)(2,1)} %get-tuple-element.43), channel_id=1, source_target_pairs={{2,0},{4,2},{6,4},{8,6},{10,8},{12,10},{14,12},{16,14},{18,16},{20... | collective-permute-start | bytes 393224 | tf_op jit(solution)/shard_map/ppermute | solution.py:17
  9.4 24.5 %collective-permute-start.1 = (bf16[128,1,512]{2,0,1:T(8,128)(2,1)}, bf16[128,1,512]{2,0,1:T(8,128)(2,1)S(1)}, u32[]{:S(2)}, u32[]{:S(2)}) collective-permute-start(bf16[128,1,512]{2,0,1:T(8,128)(2,1)} %get-tuple-element.42), channel_id=1, source_target_pairs={{0,2},{2,4},{4,6},{6,8},{8,10},{10,12},{12,14},{14,16},{16,18},{18... | collective-permute-start | bytes 393224 | tf_op jit(solution)/shard_map/ppermute | solution.py:16
  21.7 21.4 %collective-permute-start = (bf16[64,1,512]{2,0,1:T(8,128)(2,1)}, bf16[64,1,512]{2,0,1:T(8,128)(2,1)}, u32[]{:S(2)}, u32[]{:S(2)}) collective-permute-start(bf16[64,1,512]{2,0,1:T(8,128)(2,1)} %copy.102), channel_id=1, source_target_pairs={{0,254},{2,0},{4,2},{6,4},{8,6},{10,8},{12,10},{14,12},{16,14},{18... | collective-permute-start | bytes 196616 | tf_op jit(solution)/shard_map/ppermute | solution.py:24
  26.8 2.8 %copy-start.1 = (bf16[3,3,64,128]{3,2,1,0:T(8,128)(2,1)S(1)}, bf16[3,3,64,128]{3,2,1,0:T(8,128)(2,1)}, u32[]{:S(2)}) copy-start(bf16[3,3,64,128]{3,2,1,0:T(8,128)(2,1)} %param.8) | copy-start | bytes 442372
  26.9 4.8 %copy-start = (bf16[3,3,64,128]{3,2,1,0:T(8,128)(2,1)S(1)}, bf16[3,3,64,128]{3,2,1,0:T(8,128)(2,1)}, u32[]{:S(2)}) copy-start(bf16[3,3,64,128]{3,2,1,0:T(8,128)(2,1)} %param.7) | copy-start | bytes 442372
  41.1 5.6 %collective-permute-start.4 = (bf16[128,1,512]{2,0,1:T(8,128)(2,1)S(1)}, bf16[128,1,512]{2,0,1:T(8,128)(2,1)S(1)}, u32[]{:S(2)}, u32[]{:S(2)}) collective-permute-start(bf16[128,1,512]{2,0,1:T(8,128)(2,1)S(1)} %get-tuple-element.41), channel_id=1, source_target_pairs={{2,0},{4,2},{6,4},{8,6},{10,8},{12,10},{14,12},{16,14},{18,16},{20... | collective-permute-start | bytes 393224 | tf_op jit(solution)/shard_map/ppermute | solution.py:17
  41.2 7.9 %collective-permute-start.3 = (bf16[128,1,512]{2,0,1:T(8,128)(2,1)S(1)}, bf16[128,1,512]{2,0,1:T(8,128)(2,1)S(1)}, u32[]{:S(2)}, u32[]{:S(2)}) collective-permute-start(bf16[128,1,512]{2,0,1:T(8,128)(2,1)S(1)} %get-tuple-element.40), channel_id=1, source_target_pairs={{0,2},{2,4},{4,6},{6,8},{8,10},{10,12},{12,14},{14,16},{16,18},{18... | collective-permute-start | bytes 393224 | tf_op jit(solution)/shard_map/ppermute | solution.py:16
  60.5 7.2 %collective-permute-start.5 = (bf16[64,1,512]{2,0,1:T(8,128)(2,1)S(1)}, bf16[64,1,512]{2,0,1:T(8,128)(2,1)S(1)}, u32[]{:S(2)}, u32[]{:S(2)}) collective-permute-start(bf16[64,1,512]{2,0,1:T(8,128)(2,1)S(1)} %get-tuple-element.46), channel_id=1, source_target_pairs={{0,2},{2,4},{4,6},{6,8},{8,10},{10,12},{12,14},{14,16},{16,18},{18... | collective-permute-start | bytes 196616 | tf_op jit(solution)/shard_map/ppermute | solution.py:24
  60.6 7.1 %collective-permute-start.6 = (bf16[64,1,512]{2,0,1:T(8,128)(2,1)S(1)}, bf16[64,1,512]{2,0,1:T(8,128)(2,1)S(1)}, u32[]{:S(2)}, u32[]{:S(2)}) collective-permute-start(bf16[64,1,512]{2,0,1:T(8,128)(2,1)S(1)} %get-tuple-element.47), channel_id=1, source_target_pairs={{0,254},{2,0},{4,2},{6,4},{8,6},{10,8},{12,10},{14,12},{16,14},{18... | collective-permute-start | bytes 196616 | tf_op jit(solution)/shard_map/ppermute | solution.py:24
  67.0 18.7 %collective-permute-start.9 = (bf16[128,1,512]{2,0,1:T(8,128)(2,1)S(1)}, bf16[128,1,512]{2,0,1:T(8,128)(2,1)S(1)}, u32[]{:S(2)}, u32[]{:S(2)}) collective-permute-start(bf16[128,1,512]{2,0,1:T(8,128)(2,1)S(1)} %slice.526), channel_id=1, source_target_pairs={{0,2},{2,4},{4,6},{6,8},{8,10},{10,12},{12,14},{14,16},{16,18},{18... | collective-permute-start | bytes 393224 | tf_op jit(solution)/shard_map/ppermute | solution.py:24
  76.6 11.2 %collective-permute-start.7 = (bf16[64,1,512]{2,0,1:T(8,128)(2,1)S(1)}, bf16[64,1,512]{2,0,1:T(8,128)(2,1)S(1)}, u32[]{:S(2)}, u32[]{:S(2)}) collective-permute-start(bf16[64,1,512]{2,0,1:T(8,128)(2,1)S(1)} %get-tuple-element.44), channel_id=1, source_target_pairs={{0,2},{2,4},{4,6},{6,8},{8,10},{10,12},{12,14},{14,16},{16,18},{18... | collective-permute-start | bytes 196616 | tf_op jit(solution)/shard_map/ppermute | solution.py:24
  76.7 9.0 %copy-start.4 = (s32[768]{0:T(1024)S(1)}, s32[768]{0:T(1024)}, u32[]{:S(2)}) copy-start(s32[768]{0:T(1024)} %get-tuple-element.63) | copy-start | bytes 9220
  76.7 9.0 %copy-start.5 = (s32[768]{0:T(1024)S(1)}, s32[768]{0:T(1024)}, u32[]{:S(2)}) copy-start(s32[768]{0:T(1024)} %get-tuple-element.64) | copy-start | bytes 9220
  76.7 9.0 %copy-start.6 = (pred[768]{0:T(1024)(128)(4,1)S(1)}, pred[768]{0:T(1024)(128)(4,1)}, u32[]{:S(2)}) copy-start(pred[768]{0:T(1024)(128)(4,1)} %get-tuple-element.57) | copy-start | bytes 2308
  76.7 9.0 %copy-start.7 = (pred[768]{0:T(1024)(128)(4,1)S(1)}, pred[768]{0:T(1024)(128)(4,1)}, u32[]{:S(2)}) copy-start(pred[768]{0:T(1024)(128)(4,1)} %get-tuple-element.58) | copy-start | bytes 2308
  76.7 11.1 %collective-permute-start.8 = (bf16[64,1,512]{2,0,1:T(8,128)(2,1)S(1)}, bf16[64,1,512]{2,0,1:T(8,128)(2,1)S(1)}, u32[]{:S(2)}, u32[]{:S(2)}) collective-permute-start(bf16[64,1,512]{2,0,1:T(8,128)(2,1)S(1)} %get-tuple-element.45), channel_id=1, source_target_pairs={{0,254},{2,0},{4,2},{6,4},{8,6},{10,8},{12,10},{14,12},{16,14},{18... | collective-permute-start | bytes 196616 | tf_op jit(solution)/shard_map/ppermute | solution.py:24
  150.1 39.0 %all-to-all-start.1 = ((f32[128,1,2304]{2,1,0:T(1,128)}), f32[128,1,2304]{2,1,0:T(1,128)S(1)}, u32[]{:S(2)}, u32[]{:S(2)}) async-start(f32[128,1,2304]{2,1,0:T(1,128)} %broadcast_in_dim.2), calls=%async_computation.1 | async-start | bytes 2359296 | tf_op jit(solution)/shard_map/all_to_all | solution.py:163

commit v2 on v0

--- a/solution.py
+++ b/solution.py
@@ -31,6 +31,16 @@
 def widen(active):
     gathered = lax.all_gather(active, "chan", axis=0, tiled=True)
     return extended(gathered, (("blk", 1),), 1)
+
+
+def widen_by(active, before_rows, after_rows):
+    gathered = lax.all_gather(active, "chan", axis=0, tiled=True)
+    devices, length = lax.axis_size("blk"), gathered.shape[1]
+    up = [(i, (i + 1) % devices) for i in range(devices)]
+    down = [(j, i) for i, j in up]
+    before = lax.ppermute(gathered[:, length - before_rows :], "blk", up)
+    after = lax.ppermute(gathered[:, :after_rows], "blk", down)
+    return jnp.concatenate([before, gathered, after], axis=1)
 
 
 def conv_taps(padded, weight):
@@ -176,15 +186,17 @@
     mirrored = mirror[0]
     oriented = orient(inputs, mirrored)
     upstream = orient(cotangent, mirrored)
-    first_pad = widen(oriented)
-    first_pre = conv_taps(first_pad, w_first)
-    first_act = jax.nn.gelu(first_pre).astype(jnp.bfloat16)
-    second_pad = widen(first_act)
-    second_pre = conv_taps(second_pad, w_second)
-    second_act = jax.nn.gelu(second_pre).astype(jnp.bfloat16)
-    second_all = lax.all_gather(second_act, "chan", axis=0, tiled=True)
-    wrap_top = passed_along(second_all[:, -1:], "blk", 1)
-    stride_rows = jnp.concatenate([wrap_top, second_all], axis=1)
+    first_wide = widen_by(oriented, 3, 2)
+    first_pre_wide = conv_taps(first_wide, w_first)
+    first_act_wide = jax.nn.gelu(first_pre_wide).astype(jnp.bfloat16)
+    first_pad = first_wide[:, 2:-1]
+    first_pre = first_pre_wide[:, 2:-1]
+    second_wide = lax.all_gather(first_act_wide, "chan", axis=0, tiled=True)
+    second_pre_wide = conv_taps(second_wide, w_second)
+    second_act_wide = jax.nn.gelu(second_pre_wide).astype(jnp.bfloat16)
+    second_pad = second_wide[:, 1:]
+    second_pre = second_pre_wide[:, 1:]
+    stride_rows = lax.all_gather(second_act_wide, "chan", axis=0, tiled=True)
     out_rows = upstream.shape[1]
     out_cols = upstream.shape[2]
     by_parity = jnp.einsum(

time: 180 us -> 166 us (0.922)
  waiting for transfers between devices: 63.6 us -> 53.8 us
  starting transfers between devices: 47.9 us -> 41.2 us
  local copies, waits for them, and re-layouts: 13.2 us -> 16.6 us
  other arithmetic: 9.17 us -> 5.79 us
    ppermute x4 -> x2, waiting for transfers between devices: 5.05 us -> 0.01 us  [the longest x1 0.01 us: widen_by(): before = lax.ppermute(gathered[:, length - before_rows:], 'blk', up)]
    ppermute x6 -> x5, waiting for transfers between devices: 9.43 us -> 5.13 us  [passed_along(): lax.ppermute(shard, axis, [(i, (i + by) % devices) for i in range(devices)])]
    ppermute x6 -> x5, starting transfers between devices: 13.2 us -> 9.04 us  [passed_along(): lax.ppermute(shard, axis, [(i, (i + by) % devices) for i in range(devices)])]
    concatenate x2 -> x0, other arithmetic: 1.92 us -> none  [extended(): shard = jnp.concatenate([before, shard, after], axis=dim)]
    unnamed x16 -> x19, local copies, waits for them, and re-layouts: 2.89 us -> 4.46 us
    ppermute x4 -> x2, starting transfers between devices: 4.75 us -> 4.14 us  [the longest x1 2.64 us: widen_by(): after = lax.ppermute(gathered[:, :after_rows], 'blk', down)]
  transfers between devices with their start and end apart: 12 -> 9, of which waited for: 6 -> 4; matrix products, arithmetic and copies ran while one was open for 14% -> 10% of each run, Pallas kernels for 0% -> 0%
where the time goes in v2:
time: 166 us; the launch traced here: 165 us
  waiting for transfers between devices  53.8 us (32%)
  starting transfers between devices  41.2 us (25%)
  matrix products  25.7 us (15%)
  blocking collectives  19.8 us (12%)
  local copies, waits for them, and re-layouts  16.6 us (10%)
  other arithmetic  5.79 us (3%)
  between operations  2.13 us (1%)
    all_to_all x1, waiting for transfers between devices, summed_over_cycle(): pieces = lax.all_to_all(flat.reshape(devices, -1), axis, 0, 0, tiled=True)  27.3 us
    all_to_all x1, starting transfers between devices, summed_over_cycle(): pieces = lax.all_to_all(flat.reshape(devices, -1), axis, 0, 0, tiled=True)  21.7 us
    all_to_all x1, waiting for transfers between devices, summed_over_cycle(): whole = lax.all_to_all(spread, axis, 0, 0, tiled=True).reshape(-1)  21.4 us
    ppermute x5, starting transfers between devices, passed_along(): lax.ppermute(shard, axis, [(i, (i + by) % devices) for i in range(devices)])  9.04 us
    dot_general x18, matrix products, weight_taps(): jnp.einsum('orw,irw->oi', grad_out, framed[:, row_tap:row_tap + row_count...  7.29 us
    dot_general x18, matrix products, conv_taps(): jnp.einsum('oi,irw->orw', weight[row_tap, col_tap], framed[:, row_tap:row...  7.17 us
    dot_general x18, matrix products, spread_taps(): jnp.einsum('oi,orw->irw', weight[row_tap, col_tap], framed[:, row_start:r...  7.11 us
    all_to_all x1, starting transfers between devices, summed_over_cycle(): whole = lax.all_to_all(spread, axis, 0, 0, tiled=True).reshape(-1)  6.34 us
  transfers between devices with their start and end apart: 9, of which 4 were waited for; matrix products, arithmetic and copies ran while one was open for 10% of the time, Pallas kernels for 0%

profile of v2, /device:TPU:8, one launch (start us, length us, event | category | flops | bytes accessed | tf_op | source)
XLA Modules:
  0.0 165.1 jit_solution(12365107032184590398)
XLA Ops:
  2.9 2.3 %all_gather.31 = bf16[128,4,512]{2,0,1:T(8,128)(2,1)S(1)} all-gather(bf16[64,4,512]{2,0,1:T(8,128)(2,1)S(1)} %broadcast_select_fusion.1), channel_id=1, replica_groups=mesh['blk'=128,'chan'=2] {'chan'}, dimensions={0}, use_global_device_ids=true | all-gather | bytes 786432 | tf_op jit(solution)/shard_map/all_gather | solution.py:37
  6.0 1.5 collective-permute-start.1
  8.2 2.6 %collective-permute-start.2 = (bf16[128,2,512]{2,0,1:T(8,128)(2,1)}, bf16[128,2,512]{2,0,1:T(8,128)(2,1)}, u32[]{:S(2)}, u32[]{:S(2)}) collective-permute-start(bf16[128,2,512]{2,0,1:T(8,128)(2,1)} %slice.570), channel_id=1, source_target_pairs={{2,0},{4,2},{6,4},{8,6},{10,8},{12,10},{14,12},{16,14},{18,16},{20... | collective-permute-start | bytes 786440 | tf_op jit(solution)/shard_map/ppermute | solution.py:42
  11.2 2.0 %all_gather.30 = bf16[256,2,256]{0,2,1:T(8,128)(2,1)S(1)} all-gather(bf16[128,2,256]{0,2,1:T(8,128)(2,1)S(1)} %broadcast_select_fusion.2), channel_id=1, replica_groups=mesh['blk'=128,'chan'=2] {'chan'}, dimensions={0}, use_global_device_ids=true | all-gather | bytes 393216 | tf_op jit(solution)/shard_map/all_gather | solution.py:156
  13.4 2.2 %all_gather.29 = bf16[3,3,256,128]{2,3,1,0:T(8,128)(2,1)S(1)} all-gather(bf16[3,3,128,128]{2,3,1,0:T(8,128)(2,1)S(1)} %copy.62), channel_id=1, replica_groups=mesh['blk'=128,'chan'=2] {'chan'}, dimensions={2}, use_global_device_ids=true | all-gather | bytes 884736 | tf_op jit(solution)/shard_map/all_gather | solution.py:145
  19.2 2.3 %reshape.57 = f32[64,6,514]{0,2,1:T(8,128)} reshape(f32[64,3,2,257,2]{0,4,3,2,1:T(2,128)S(1)} %copy.65) | data formatting | bytes 1579008 | tf_op jit(solution)/shard_map/reshape | solution.py:127
  26.5 2.0 %all_gather.28 = bf16[3,3,128,128]{3,2,1,0:T(8,128)(2,1)S(1)} all-gather(bf16[3,3,64,128]{3,2,1,0:T(8,128)(2,1)S(1)} %copy-done.1), channel_id=1, replica_groups=mesh['blk'=128,'chan'=2] {'chan'}, dimensions={2}, use_global_device_ids=true | all-gather | bytes 442368 | tf_op jit(solution)/shard_map/all_gather | solution.py:145
  34.8 2.6 %all_gather.32 = bf16[128,7,512]{2,0,1:T(8,128)(2,1)S(1)} all-gather(bf16[64,7,512]{2,0,1:T(8,128)(2,1)S(1)} %get-tuple-element.41), channel_id=1, replica_groups=mesh['blk'=128,'chan'=2] {'chan'}, dimensions={0}, use_global_device_ids=true | all-gather | bytes 1376256 | tf_op jit(solution)/shard_map/all_gather | solution.py:194
  41.2 2.2 %all_gather.33 = bf16[128,4,512]{2,0,1:T(8,128)(2,1)S(1)} all-gather(bf16[64,4,512]{2,0,1:T(8,128)(2,1)S(1)} %fusion.63), channel_id=1, replica_groups=mesh['blk'=128,'chan'=2] {'chan'}, dimensions={0}, use_global_device_ids=true | all-gather | bytes 786432 | tf_op jit(solution)/shard_map/all_gather | solution.py:151
  46.6 2.3 %all_gather.35 = bf16[128,5,512]{2,0,1:T(8,128)(2,1)S(1)} all-gather(bf16[64,5,512]{2,0,1:T(8,128)(2,1)S(1)} %get-tuple-element.47), channel_id=1, replica_groups=mesh['blk'=128,'chan'=2] {'chan'}, dimensions={0}, use_global_device_ids=true | all-gather | bytes 983040 | tf_op jit(solution)/shard_map/all_gather | solution.py:199
  54.5 1.6 collective-permute-start.3
  56.1 2.6 %collective-permute-start.4 = (bf16[64,1,512]{2,0,1:T(8,128)(2,1)S(1)}, bf16[64,1,512]{2,0,1:T(8,128)(2,1)S(1)}, u32[]{:S(2)}, u32[]{:S(2)}) collective-permute-start(bf16[64,1,512]{2,0,1:T(8,128)(2,1)S(1)} %get-tuple-element.35), channel_id=1, source_target_pairs={{0,254},{2,0},{4,2},{6,4},{8,6},{10,8},{12,10},{14,12},{16,14},{18... | collective-permute-start | bytes 196616 | tf_op jit(solution)/shard_map/ppermute | solution.py:24
  58.9 2.0 %collective-permute-done.3 = bf16[64,1,512]{2,0,1:T(8,128)(2,1)S(1)} collective-permute-done((bf16[64,1,512]{2,0,1:T(8,128)(2,1)S(1)}, bf16[64,1,512]{2,0,1:T(8,128)(2,1)S(1)}, u32[]{:S(2)}, u32[]{:S(2)}) %collective-permute-start.3) | collective-permute-done | bytes 65568 | tf_op jit(solution)/shard_map/ppermute | solution.py:24
  66.7 21.7 %all-to-all-start = ((f32[128,1,2304]{2,1,0:T(1,128)}), f32[128,1,2304]{2,1,0:T(1,128)S(1)}, u32[]{:S(2)}, u32[]{:S(2)}) async-start(f32[128,1,2304]{2,1,0:T(1,128)} %bitcast.162), calls=%async_computation | async-start | bytes 2359296 | tf_op jit(solution)/shard_map/all_to_all | solution.py:170
  88.4 2.0 %all_gather.27 = bf16[3,3,128,128]{3,2,1,0:T(8,128)(2,1)S(1)} all-gather(bf16[3,3,64,128]{3,2,1,0:T(8,128)(2,1)S(1)} %copy-done.2), channel_id=1, replica_groups=mesh['blk'=128,'chan'=2] {'chan'}, dimensions={2}, use_global_device_ids=true | all-gather | bytes 442368 | tf_op jit(solution)/shard_map/all_gather | solution.py:145
  90.4 2.2 %all_gather.34 = bf16[128,4,512]{2,0,1:T(8,128)(2,1)S(1)} all-gather(bf16[64,4,512]{2,0,1:T(8,128)(2,1)S(1)} %fusion.70), channel_id=1, replica_groups=mesh['blk'=128,'chan'=2] {'chan'}, dimensions={0}, use_global_device_ids=true | all-gather | bytes 786432 | tf_op jit(solution)/shard_map/all_gather | solution.py:151
  93.8 27.3 %all-to-all-done = f32[128,1,2304]{2,1,0:T(1,128)S(1)} async-done(((f32[128,1,2304]{2,1,0:T(1,128)}), f32[128,1,2304]{2,1,0:T(1,128)S(1)}, u32[]{:S(2)}, u32[]{:S(2)}) %all-to-all-start) | async-done | bytes 1179680 | tf_op jit(solution)/shard_map/all_to_all | solution.py:170
  121.8 1.6 broadcast_in_dim.2
  123.4 6.3 %all-to-all-start.1 = ((f32[128,1,2304]{2,1,0:T(1,128)}), f32[128,1,2304]{2,1,0:T(1,128)S(1)}, u32[]{:S(2)}, u32[]{:S(2)}) async-start(f32[128,1,2304]{2,1,0:T(1,128)} %broadcast_in_dim.2), calls=%async_computation.1 | async-start | bytes 2359296 | tf_op jit(solution)/shard_map/all_to_all | solution.py:173
  132.2 1.5 collective-permute-start.5
  133.7 2.7 %collective-permute-start.6 = (bf16[64,1,512]{2,0,1:T(8,128)(2,1)S(1)}, bf16[64,1,512]{2,0,1:T(8,128)(2,1)S(1)}, u32[]{:S(2)}, u32[]{:S(2)}) collective-permute-start(bf16[64,1,512]{2,0,1:T(8,128)(2,1)S(1)} %get-tuple-element.33), channel_id=1, source_target_pairs={{0,254},{2,0},{4,2},{6,4},{8,6},{10,8},{12,10},{14,12},{16,14},{18... | collective-permute-start | bytes 196616 | tf_op jit(solution)/shard_map/ppermute | solution.py:24
  136.4 3.1 %collective-permute-done.5 = bf16[64,1,512]{2,0,1:T(8,128)(2,1)S(1)} collective-permute-done((bf16[64,1,512]{2,0,1:T(8,128)(2,1)S(1)}, bf16[64,1,512]{2,0,1:T(8,128)(2,1)S(1)}, u32[]{:S(2)}, u32[]{:S(2)}) %collective-permute-start.5) | collective-permute-done | bytes 65568 | tf_op jit(solution)/shard_map/ppermute | solution.py:24
  141.1 21.4 %all-to-all-done.1 = f32[128,1,2304]{2,1,0:T(1,128)S(1)} async-done(((f32[128,1,2304]{2,1,0:T(1,128)}), f32[128,1,2304]{2,1,0:T(1,128)S(1)}, u32[]{:S(2)}, u32[]{:S(2)}) %all-to-all-start.1) | async-done | bytes 1179680 | tf_op jit(solution)/shard_map/all_to_all | solution.py:173
  162.4 1.4 slice_multiply_fusion.1
  (138 shorter events, 43.5 us)
Async XLA Ops:
  0.6 2.2 %copy-start = (bf16[64,4,512]{2,1,0:T(4,128)(2,1)S(1)}, bf16[64,4,512]{2,1,0:T(4,128)(2,1)}, u32[]{:S(2)}) copy-start(bf16[64,4,512]{2,1,0:T(4,128)(2,1)} %param.6) | copy-start | bytes 786436
  2.9 8.0 %copy-start.4 = (bf16[128,2,256]{2,1,0:T(2,128)(2,1)S(1)}, bf16[128,2,256]{2,1,0:T(2,128)(2,1)}, u32[]{:S(2)}) copy-start(bf16[128,2,256]{2,1,0:T(2,128)(2,1)} %param.10) | copy-start | bytes 393220
  5.2 8.0 %copy-start.3 = (bf16[3,3,128,128]{3,2,1,0:T(8,128)(2,1)S(1)}, bf16[3,3,128,128]{3,2,1,0:T(8,128)(2,1)}, u32[]{:S(2)}) copy-start(bf16[3,3,128,128]{3,2,1,0:T(8,128)(2,1)} %param.9) | copy-start | bytes 884740
  6.0 22.5 %collective-permute-start.1 = (bf16[128,3,512]{2,0,1:T(8,128)(2,1)}, bf16[128,3,512]{2,0,1:T(8,128)(2,1)}, u32[]{:S(2)}, u32[]{:S(2)}) collective-permute-start(bf16[128,3,512]{2,0,1:T(8,128)(2,1)} %slice.569), channel_id=1, source_target_pairs={{0,2},{2,4},{4,6},{6,8},{8,10},{10,12},{12,14},{14,16},{16,18},{18... | collective-permute-start | bytes 1179656 | tf_op jit(solution)/shard_map/ppermute | solution.py:41
  8.2 21.5 %collective-permute-start.2 = (bf16[128,2,512]{2,0,1:T(8,128)(2,1)}, bf16[128,2,512]{2,0,1:T(8,128)(2,1)}, u32[]{:S(2)}, u32[]{:S(2)}) collective-permute-start(bf16[128,2,512]{2,0,1:T(8,128)(2,1)} %slice.570), channel_id=1, source_target_pairs={{2,0},{4,2},{6,4},{8,6},{10,8},{12,10},{14,12},{16,14},{18,16},{20... | collective-permute-start | bytes 786440 | tf_op jit(solution)/shard_map/ppermute | solution.py:42
  22.6 6.0 %collective-permute-start = (bf16[64,1,512]{2,0,1:T(8,128)(2,1)S(1)}, bf16[64,1,512]{2,0,1:T(8,128)(2,1)S(1)}, u32[]{:S(2)}, u32[]{:S(2)}) collective-permute-start(bf16[64,1,512]{2,0,1:T(8,128)(2,1)S(1)} %copy.102), channel_id=1, source_target_pairs={{0,254},{2,0},{4,2},{6,4},{8,6},{10,8},{12,10},{14,12},{16,14},{18... | collective-permute-start | bytes 196616 | tf_op jit(solution)/shard_map/ppermute | solution.py:24
  25.6 0.9 copy-start.1
  29.6 1.1 copy-start.2
  54.5 6.5 %collective-permute-start.3 = (bf16[64,1,512]{2,0,1:T(8,128)(2,1)S(1)}, bf16[64,1,512]{2,0,1:T(8,128)(2,1)S(1)}, u32[]{:S(2)}, u32[]{:S(2)}) collective-permute-start(bf16[64,1,512]{2,0,1:T(8,128)(2,1)S(1)} %get-tuple-element.34), channel_id=1, source_target_pairs={{0,2},{2,4},{4,6},{6,8},{8,10},{10,12},{12,14},{14,16},{16,18},{18... | collective-permute-start | bytes 196616 | tf_op jit(solution)/shard_map/ppermute | solution.py:24
  56.1 4.9 %collective-permute-start.4 = (bf16[64,1,512]{2,0,1:T(8,128)(2,1)S(1)}, bf16[64,1,512]{2,0,1:T(8,128)(2,1)S(1)}, u32[]{:S(2)}, u32[]{:S(2)}) collective-permute-start(bf16[64,1,512]{2,0,1:T(8,128)(2,1)S(1)} %get-tuple-element.35), channel_id=1, source_target_pairs={{0,254},{2,0},{4,2},{6,4},{8,6},{10,8},{12,10},{14,12},{16,14},{18... | collective-permute-start | bytes 196616 | tf_op jit(solution)/shard_map/ppermute | solution.py:24
  66.7 54.4 %all-to-all-start = ((f32[128,1,2304]{2,1,0:T(1,128)}), f32[128,1,2304]{2,1,0:T(1,128)S(1)}, u32[]{:S(2)}, u32[]{:S(2)}) async-start(f32[128,1,2304]{2,1,0:T(1,128)} %bitcast.162), calls=%async_computation | async-start | bytes 2359296 | tf_op jit(solution)/shard_map/all_to_all | solution.py:170
  123.4 39.0 %all-to-all-start.1 = ((f32[128,1,2304]{2,1,0:T(1,128)}), f32[128,1,2304]{2,1,0:T(1,128)S(1)}, u32[]{:S(2)}, u32[]{:S(2)}) async-start(f32[128,1,2304]{2,1,0:T(1,128)} %broadcast_in_dim.2), calls=%async_computation.1 | async-start | bytes 2359296 | tf_op jit(solution)/shard_map/all_to_all | solution.py:173
  132.2 7.3 %collective-permute-start.5 = (bf16[64,1,512]{2,0,1:T(8,128)(2,1)S(1)}, bf16[64,1,512]{2,0,1:T(8,128)(2,1)S(1)}, u32[]{:S(2)}, u32[]{:S(2)}) collective-permute-start(bf16[64,1,512]{2,0,1:T(8,128)(2,1)S(1)} %get-tuple-element.32), channel_id=1, source_target_pairs={{0,2},{2,4},{4,6},{6,8},{8,10},{10,12},{12,14},{14,16},{16,18},{18... | collective-permute-start | bytes 196616 | tf_op jit(solution)/shard_map/ppermute | solution.py:24
  133.7 5.8 %collective-permute-start.6 = (bf16[64,1,512]{2,0,1:T(8,128)(2,1)S(1)}, bf16[64,1,512]{2,0,1:T(8,128)(2,1)S(1)}, u32[]{:S(2)}, u32[]{:S(2)}) collective-permute-start(bf16[64,1,512]{2,0,1:T(8,128)(2,1)S(1)} %get-tuple-element.33), channel_id=1, source_target_pairs={{0,254},{2,0},{4,2},{6,4},{8,6},{10,8},{12,10},{14,12},{16,14},{18... | collective-permute-start | bytes 196616 | tf_op jit(solution)/shard_map/ppermute | solution.py:24

commit v3 on v2

--- a/solution.py
+++ b/solution.py
@@ -141,10 +141,18 @@
     return jnp.concatenate([interior[:, :-1], interior[:, -1:] + from_next], axis=1)
 
 
-def own_inputs(weight):
-    whole = lax.all_gather(weight, "chan", axis=2, tiled=True)
-    width = whole.shape[3] // lax.axis_size("chan")
-    return lax.dynamic_slice_in_dim(whole, lax.axis_index("chan") * width, width, axis=3)
+def own_inputs(weights):
+    sizes = [w.shape[2] for w in weights]
+    devices = lax.axis_size("chan")
+    whole = lax.all_gather(jnp.concatenate(weights, axis=2), "chan", axis=0, tiled=False)
+    width = weights[0].shape[3] // devices
+    mine = lax.dynamic_slice_in_dim(whole, lax.axis_index("chan") * width, width, axis=4)
+    out, start = [], 0
+    for size in sizes:
+        parts = [mine[d, :, :, start : start + size] for d in range(devices)]
+        out.append(jnp.concatenate(parts, axis=2))
+        start += size
+    return out
 
 
 def input_grad(delta, weight):
@@ -223,13 +231,14 @@
         ],
         axis=1,
     )
-    second_back = third_input_grad(upstream, own_inputs(w_third))
+    first_mine, second_mine, third_mine = own_inputs((w_first, w_second, w_third))
+    second_back = third_input_grad(upstream, third_mine)
     second_delta = gelu_back(second_pre, second_back).astype(jnp.bfloat16)
     second_grad = weight_taps(second_delta, second_pad)
-    first_back = input_grad(second_delta, own_inputs(w_second))
+    first_back = input_grad(second_delta, second_mine)
     first_delta = gelu_back(first_pre, first_back).astype(jnp.bfloat16)
     first_grad = weight_taps(first_delta, first_pad)
-    input_back = input_grad(first_delta, own_inputs(w_first)).astype(jnp.bfloat16)
+    input_back = input_grad(first_delta, first_mine).astype(jnp.bfloat16)
     reduced = summed_over_cycle((first_grad, second_grad, third_grad), "blk")
     cell_count = inputs.shape[1] * inputs.shape[2] * lax.axis_size("blk")
     return (

time: 166 us -> 199 us (1.20)
  between operations: 2.13 us -> 15.6 us
  waiting for transfers between devices: 53.8 us -> 64.5 us
  local copies, waits for them, and re-layouts: 16.6 us -> 27.2 us
  blocking collectives: 19.8 us -> 13.9 us
  starting transfers between devices: 41.2 us -> 43.6 us
    all_gather x3 -> x0, blocking collectives: 6.25 us -> none  [own_inputs(): whole = lax.all_gather(weight, 'chan', axis=2, tiled=True)]
    ppermute x1, waiting for transfers between devices: 0.01 us -> 5.53 us  [widen_by(): before = lax.ppermute(gathered[:, length - before_rows:], 'blk', up)]
    ppermute x5, waiting for transfers between devices: 5.13 us -> 7.72 us  [passed_along(): lax.ppermute(shard, axis, [(i, (i + by) % devices) for i in range(devices)])]
    another operation x1, local copies, waits for them, and re-layouts: 1.11 us -> 3.57 us  [spread_stride(): woven = jnp.stack(parity_rows, axis=2)]
    unnamed x19 -> x34, local copies, waits for them, and re-layouts: 4.46 us -> 6.88 us
    all_gather x0 -> x1, local copies, waits for them, and re-layouts: none -> 2.38 us  [own_inputs(): lax.all_gather(jnp.concatenate(weights, axis=2), 'chan', axis=0, tiled=Fa...]
    all_to_all x1, waiting for transfers between devices: 27.3 us -> 29.7 us  [summed_over_cycle(): pieces = lax.all_to_all(flat.reshape(devices, -1), axis, 0, 0, tiled=True)]
    squeeze x0 -> x2, local copies, waits for them, and re-layouts: none -> 2.32 us  [own_inputs(): parts = [mine[d, :, :, start:start + size] for d in range(devices)]]
  transfers between devices with their start and end apart: 9 -> 10, of which waited for: 4 -> 6; matrix products, arithmetic and copies ran while one was open for 10% -> 10% of each run, Pallas kernels for 0% -> 0%
where the time goes in v3:
time: 199 us; the launch traced here: 198 us
  waiting for transfers between devices  64.5 us (32%)
  starting transfers between devices  43.6 us (22%)
  local copies, waits for them, and re-layouts  27.2 us (14%)
  matrix products  26 us (13%)
  between operations  15.6 us (8%)
  blocking collectives  13.9 us (7%)
  other arithmetic  7.72 us (4%)
    all_to_all x1, waiting for transfers between devices, summed_over_cycle(): pieces = lax.all_to_all(flat.reshape(devices, -1), axis, 0, 0, tiled=True)  29.7 us
    all_to_all x1, starting transfers between devices, summed_over_cycle(): pieces = lax.all_to_all(flat.reshape(devices, -1), axis, 0, 0, tiled=True)  23.8 us
    all_to_all x1, waiting for transfers between devices, summed_over_cycle(): whole = lax.all_to_all(spread, axis, 0, 0, tiled=True).reshape(-1)  21.5 us
    ppermute x5, starting transfers between devices, passed_along(): lax.ppermute(shard, axis, [(i, (i + by) % devices) for i in range(devices)])  9.09 us
    dot_general x18, matrix products, conv_taps(): jnp.einsum('oi,irw->orw', weight[row_tap, col_tap], framed[:, row_tap:row...  8.92 us
    ppermute x5, waiting for transfers between devices, passed_along(): lax.ppermute(shard, axis, [(i, (i + by) % devices) for i in range(devices)])  7.72 us
    unnamed x34, local copies, waits for them, and re-layouts  6.88 us
    dot_general x18, matrix products, spread_taps(): jnp.einsum('oi,orw->irw', weight[row_tap, col_tap], framed[:, row_start:r...  6.6 us
  transfers between devices with their start and end apart: 10, of which 6 were waited for; matrix products, arithmetic and copies ran while one was open for 10% of the time, Pallas kernels for 0%

profile of v3, /device:TPU:8, one launch (start us, length us, event | category | flops | bytes accessed | tf_op | source)
XLA Modules:
  0.0 198.4 jit_solution(569394439884662489)
XLA Ops:
  9.5 2.3 %all_gather.27 = bf16[128,4,512]{2,0,1:T(8,128)(2,1)S(1)} all-gather(bf16[64,4,512]{2,0,1:T(8,128)(2,1)S(1)} %broadcast_select_fusion.1), channel_id=1, replica_groups=mesh['blk'=128,'chan'=2] {'chan'}, dimensions={0}, use_global_device_ids=true | all-gather | bytes 786432 | tf_op jit(solution)/shard_map/all_gather | solution.py:37
  13.5 2.7 %collective-permute-start.2 = (bf16[128,2,512]{2,0,1:T(8,128)(2,1)S(1)}, bf16[128,2,512]{2,0,1:T(8,128)(2,1)S(1)}, u32[]{:S(2)}, u32[]{:S(2)}) collective-permute-start(bf16[128,2,512]{2,0,1:T(8,128)(2,1)S(1)} %slice.614), channel_id=1, source_target_pairs={{2,0},{4,2},{6,4},{8,6},{10,8},{12,10},{14,12},{16,14},{18,16},{20... | collective-permute-start | bytes 786440 | tf_op jit(solution)/shard_map/ppermute | solution.py:42
  17.4 2.0 %all_gather.26 = bf16[256,2,256]{0,2,1:T(8,128)(2,1)S(1)} all-gather(bf16[128,2,256]{0,2,1:T(8,128)(2,1)S(1)} %broadcast_select_fusion.2), channel_id=1, replica_groups=mesh['blk'=128,'chan'=2] {'chan'}, dimensions={0}, use_global_device_ids=true | all-gather | bytes 393216 | tf_op jit(solution)/shard_map/all_gather | solution.py:164
  19.7 5.5 %collective-permute-done.1 = bf16[128,3,512]{2,0,1:T(8,128)(2,1)S(1)} collective-permute-done((bf16[128,3,512]{2,0,1:T(8,128)(2,1)S(1)}, bf16[128,3,512]{2,0,1:T(8,128)(2,1)S(1)}, u32[]{:S(2)}, u32[]{:S(2)}) %collective-permute-start.1) | collective-permute-done | bytes 393248 | tf_op jit(solution)/shard_map/ppermute | solution.py:41
  28.9 1.8 fusion.30
  30.6 2.7 %all_gather.28 = bf16[128,7,512]{2,0,1:T(8,128)(2,1)S(1)} all-gather(bf16[64,7,512]{2,0,1:T(8,128)(2,1)S(1)} %get-tuple-element.47), channel_id=1, replica_groups=mesh['blk'=128,'chan'=2] {'chan'}, dimensions={0}, use_global_device_ids=true | all-gather | bytes 1376256 | tf_op jit(solution)/shard_map/all_gather | solution.py:202
  37.5 2.4 %all_gather.31 = bf16[128,5,512]{2,0,1:T(8,128)(2,1)S(1)} all-gather(bf16[64,5,512]{2,0,1:T(8,128)(2,1)S(1)} %get-tuple-element.53), channel_id=1, replica_groups=mesh['blk'=128,'chan'=2] {'chan'}, dimensions={0}, use_global_device_ids=true | all-gather | bytes 983040 | tf_op jit(solution)/shard_map/all_gather | solution.py:207
  43.1 2.4 %copy.52 = bf16[6,3,256,128]{2,3,1,0:T(8,128)(2,1)} copy(bf16[6,3,256,128]{3,2,1,0:T(8,128)(2,1)} %all-gather.3.cloned.1.call-done) | data formatting | bytes 2359296 | tf_op jit(solution)/shard_map/all_gather | solution.py:147
  49.9 3.6 %copy.55 = f32[64,3,2,257,2]{0,4,3,2,1:T(2,128)} copy(f32[64,3,2,257,2]{3,0,1,4,2:T(8,128)} %pad_maximum_fusion) | data formatting | bytes 1579008 | tf_op jit(solution)/shard_map/stack | solution.py:126
  53.5 3.2 %reshape.57 = f32[64,6,514]{0,2,1:T(8,128)} reshape(f32[64,3,2,257,2]{0,4,3,2,1:T(2,128)} %copy.55) | data formatting | bytes 1579008 | tf_op jit(solution)/shard_map/reshape | solution.py:127
  56.6 2.1 %slice.610 = f32[64,3,512]{0,2,1:T(8,128)} slice(f32[64,6,514]{0,2,1:T(8,128)} %reshape.57), slice={[0:64], [1:4], [1:513]} | slice | bytes 786432 | tf_op jit(solution)/shard_map/slice | solution.py:141
  61.3 2.1 %copy.70 = f32[64,3,512]{2,0,1:T(8,128)} copy(f32[64,3,512]{0,2,1:T(8,128)} %slice.610) | data formatting | bytes 786432
  66.6 2.4 %collective-permute-done = bf16[64,1,512]{2,0,1:T(8,128)(2,1)S(1)} collective-permute-done((bf16[64,1,512]{2,0,1:T(8,128)(2,1)S(1)}, bf16[64,1,512]{2,0,1:T(8,128)(2,1)S(1)}, u32[]{:S(2)}, u32[]{:S(2)}) %collective-permute-start) | collective-permute-done | bytes 65568 | tf_op jit(solution)/shard_map/ppermute | solution.py:24
  69.4 2.2 %all_gather.29 = bf16[128,4,512]{2,0,1:T(8,128)(2,1)S(1)} all-gather(bf16[64,4,512]{2,0,1:T(8,128)(2,1)S(1)} %fusion.63), channel_id=1, replica_groups=mesh['blk'=128,'chan'=2] {'chan'}, dimensions={0}, use_global_device_ids=true | all-gather | bytes 786432 | tf_op jit(solution)/shard_map/all_gather | solution.py:159
  78.3 4.1 %collective-permute-start.4 = (bf16[64,1,512]{2,0,1:T(8,128)(2,1)S(1)}, bf16[64,1,512]{2,0,1:T(8,128)(2,1)S(1)}, u32[]{:S(2)}, u32[]{:S(2)}) collective-permute-start(bf16[64,1,512]{2,0,1:T(8,128)(2,1)S(1)} %get-tuple-element.41), channel_id=1, source_target_pairs={{0,254},{2,0},{4,2},{6,4},{8,6},{10,8},{12,10},{14,12},{16,14},{18... | collective-permute-start | bytes 196616 | tf_op jit(solution)/shard_map/ppermute | solution.py:24
  82.5 2.1 %collective-permute-done.3 = bf16[64,1,512]{2,0,1:T(8,128)(2,1)S(1)} collective-permute-done((bf16[64,1,512]{2,0,1:T(8,128)(2,1)S(1)}, bf16[64,1,512]{2,0,1:T(8,128)(2,1)S(1)}, u32[]{:S(2)}, u32[]{:S(2)}) %collective-permute-start.3) | collective-permute-done | bytes 65568 | tf_op jit(solution)/shard_map/ppermute | solution.py:24
  90.6 23.8 %all-to-all-start = ((f32[128,1,2304]{2,1,0:T(1,128)}), f32[128,1,2304]{2,1,0:T(1,128)S(1)}, u32[]{:S(2)}, u32[]{:S(2)}) async-start(f32[128,1,2304]{2,1,0:T(1,128)} %bitcast.393), calls=%async_computation | async-start | bytes 2359296 | tf_op jit(solution)/shard_map/all_to_all | solution.py:178
  114.4 2.2 %all_gather.30 = bf16[128,4,512]{2,0,1:T(8,128)(2,1)S(1)} all-gather(bf16[64,4,512]{2,0,1:T(8,128)(2,1)S(1)} %fusion.70), channel_id=1, replica_groups=mesh['blk'=128,'chan'=2] {'chan'}, dimensions={0}, use_global_device_ids=true | all-gather | bytes 786432 | tf_op jit(solution)/shard_map/all_gather | solution.py:159
  117.7 29.7 %all-to-all-done = f32[128,1,2304]{2,1,0:T(1,128)S(1)} async-done(((f32[128,1,2304]{2,1,0:T(1,128)}), f32[128,1,2304]{2,1,0:T(1,128)S(1)}, u32[]{:S(2)}, u32[]{:S(2)}) %all-to-all-start) | async-done | bytes 1179680 | tf_op jit(solution)/shard_map/all_to_all | solution.py:178
  148.1 1.6 broadcast_in_dim.2
  149.8 6.3 %all-to-all-start.1 = ((f32[128,1,2304]{2,1,0:T(1,128)}), f32[128,1,2304]{2,1,0:T(1,128)S(1)}, u32[]{:S(2)}, u32[]{:S(2)}) async-start(f32[128,1,2304]{2,1,0:T(1,128)} %broadcast_in_dim.2), calls=%async_computation.1 | async-start | bytes 2359296 | tf_op jit(solution)/shard_map/all_to_all | solution.py:181
  159.9 2.7 %collective-permute-start.6 = (bf16[64,1,512]{2,0,1:T(8,128)(2,1)S(1)}, bf16[64,1,512]{2,0,1:T(8,128)(2,1)S(1)}, u32[]{:S(2)}, u32[]{:S(2)}) collective-permute-start(bf16[64,1,512]{2,0,1:T(8,128)(2,1)S(1)} %get-tuple-element.39), channel_id=1, source_target_pairs={{0,254},{2,0},{4,2},{6,4},{8,6},{10,8},{12,10},{14,12},{16,14},{18... | collective-permute-start | bytes 196616 | tf_op jit(solution)/shard_map/ppermute | solution.py:24
  162.6 3.2 %collective-permute-done.5 = bf16[64,1,512]{2,0,1:T(8,128)(2,1)S(1)} collective-permute-done((bf16[64,1,512]{2,0,1:T(8,128)(2,1)S(1)}, bf16[64,1,512]{2,0,1:T(8,128)(2,1)S(1)}, u32[]{:S(2)}, u32[]{:S(2)}) %collective-permute-start.5) | collective-permute-done | bytes 65568 | tf_op jit(solution)/shard_map/ppermute | solution.py:24
  167.3 21.5 %all-to-all-done.1 = f32[128,1,2304]{2,1,0:T(1,128)S(1)} async-done(((f32[128,1,2304]{2,1,0:T(1,128)}), f32[128,1,2304]{2,1,0:T(1,128)S(1)}, u32[]{:S(2)}, u32[]{:S(2)}) %all-to-all-start.1) | async-done | bytes 1179680 | tf_op jit(solution)/shard_map/all_to_all | solution.py:181
  (157 shorter events, 48.1 us)
Async XLA Ops:
  7.2 2.2 %copy-start.6 = (bf16[64,4,512]{2,1,0:T(4,128)(2,1)S(1)}, bf16[64,4,512]{2,1,0:T(4,128)(2,1)}, u32[]{:S(2)}) copy-start(bf16[64,4,512]{2,1,0:T(4,128)(2,1)} %param.6) | copy-start | bytes 786436
  7.2 35.9 %all-gather.3.cloned.1.call-start = ((), (), s32[]{:S(2)}) async-start(), calls=%async_computation.2 | async-start | bytes 1769472 | tf_op jit(solution)/shard_map/all_gather | solution.py:147
  9.5 6.7 %copy-start.9 = (bf16[3,3,64,128]{3,2,1,0:T(8,128)(2,1)S(1)}, bf16[3,3,64,128]{3,2,1,0:T(8,128)(2,1)}, u32[]{:S(2)}) copy-start(bf16[3,3,64,128]{3,2,1,0:T(8,128)(2,1)} %param.7) | copy-start | bytes 442372
  9.5 6.7 %copy-start.10 = (bf16[3,3,64,128]{3,2,1,0:T(8,128)(2,1)S(1)}, bf16[3,3,64,128]{3,2,1,0:T(8,128)(2,1)}, u32[]{:S(2)}) copy-start(bf16[3,3,64,128]{3,2,1,0:T(8,128)(2,1)} %param.8) | copy-start | bytes 442372
  9.5 6.7 %copy-start.11 = (bf16[3,3,128,128]{3,2,1,0:T(8,128)(2,1)S(1)}, bf16[3,3,128,128]{3,2,1,0:T(8,128)(2,1)}, u32[]{:S(2)}) copy-start(bf16[3,3,128,128]{3,2,1,0:T(8,128)(2,1)} %param.9) | copy-start | bytes 884740
  11.9 5.2 %copy-start.12 = (bf16[128,2,256]{2,1,0:T(2,128)(2,1)S(1)}, bf16[128,2,256]{2,1,0:T(2,128)(2,1)}, u32[]{:S(2)}) copy-start(bf16[128,2,256]{2,1,0:T(2,128)(2,1)} %param.10) | copy-start | bytes 393220
  11.9 13.3 %collective-permute-start.1 = (bf16[128,3,512]{2,0,1:T(8,128)(2,1)S(1)}, bf16[128,3,512]{2,0,1:T(8,128)(2,1)S(1)}, u32[]{:S(2)}, u32[]{:S(2)}) collective-permute-start(bf16[128,3,512]{2,0,1:T(8,128)(2,1)S(1)} %slice.613), channel_id=1, source_target_pairs={{0,2},{2,4},{4,6},{6,8},{8,10},{10,12},{12,14},{14,16},{16,18},{18... | collective-permute-start | bytes 1179656 | tf_op jit(solution)/shard_map/ppermute | solution.py:41
  13.5 11.9 %collective-permute-start.2 = (bf16[128,2,512]{2,0,1:T(8,128)(2,1)S(1)}, bf16[128,2,512]{2,0,1:T(8,128)(2,1)S(1)}, u32[]{:S(2)}, u32[]{:S(2)}) collective-permute-start(bf16[128,2,512]{2,0,1:T(8,128)(2,1)S(1)} %slice.614), channel_id=1, source_target_pairs={{2,0},{4,2},{6,4},{8,6},{10,8},{12,10},{14,12},{16,14},{18,16},{20... | collective-permute-start | bytes 786440 | tf_op jit(solution)/shard_map/ppermute | solution.py:42
  25.4 3.2 %copy-start = (bf16[128,7,512]{2,0,1:T(8,128)(2,1)}, bf16[128,7,512]{2,0,1:T(8,128)(2,1)S(1)}, u32[]{:S(2)}) copy-start(bf16[128,7,512]{2,0,1:T(8,128)(2,1)S(1)} %get-tuple-element.36) | copy-start | bytes 2752516
  25.4 0.8 copy-start.7
  64.6 4.4 %copy-start.4 = (f32[64,5,512]{2,0,1:T(8,128)S(1)}, f32[64,5,512]{2,0,1:T(8,128)}, u32[]{:S(2)}) copy-start(f32[64,5,512]{2,0,1:T(8,128)} %get-tuple-element.54) | copy-start | bytes 1966084
  64.6 4.4 %copy-start.5 = (f32[64,3,512]{2,0,1:T(8,128)S(1)}, f32[64,3,512]{2,0,1:T(8,128)}, u32[]{:S(2)}) copy-start(f32[64,3,512]{2,0,1:T(8,128)} %copy.70) | copy-start | bytes 1179652
  64.6 4.4 %collective-permute-start = (bf16[64,1,512]{2,0,1:T(8,128)(2,1)S(1)}, bf16[64,1,512]{2,0,1:T(8,128)(2,1)S(1)}, u32[]{:S(2)}, u32[]{:S(2)}) collective-permute-start(bf16[64,1,512]{2,0,1:T(8,128)(2,1)S(1)} %copy.72), channel_id=1, source_target_pairs={{0,254},{2,0},{4,2},{6,4},{8,6},{10,8},{12,10},{14,12},{16,14},{18... | collective-permute-start | bytes 196616 | tf_op jit(solution)/shard_map/ppermute | solution.py:24
  78.2 6.5 %collective-permute-start.3 = (bf16[64,1,512]{2,0,1:T(8,128)(2,1)S(1)}, bf16[64,1,512]{2,0,1:T(8,128)(2,1)S(1)}, u32[]{:S(2)}, u32[]{:S(2)}) collective-permute-start(bf16[64,1,512]{2,0,1:T(8,128)(2,1)S(1)} %get-tuple-element.40), channel_id=1, source_target_pairs={{0,2},{2,4},{4,6},{6,8},{8,10},{10,12},{12,14},{14,16},{16,18},{18... | collective-permute-start | bytes 196616 | tf_op jit(solution)/shard_map/ppermute | solution.py:24
  78.3 6.4 %collective-permute-start.4 = (bf16[64,1,512]{2,0,1:T(8,128)(2,1)S(1)}, bf16[64,1,512]{2,0,1:T(8,128)(2,1)S(1)}, u32[]{:S(2)}, u32[]{:S(2)}) collective-permute-start(bf16[64,1,512]{2,0,1:T(8,128)(2,1)S(1)} %get-tuple-element.41), channel_id=1, source_target_pairs={{0,254},{2,0},{4,2},{6,4},{8,6},{10,8},{12,10},{14,12},{16,14},{18... | collective-permute-start | bytes 196616 | tf_op jit(solution)/shard_map/ppermute | solution.py:24
  82.4 2.3 %copy-start.3 = (f32[64,7,512]{2,0,1:T(8,128)S(1)}, f32[64,7,512]{2,0,1:T(8,128)}, u32[]{:S(2)}) copy-start(f32[64,7,512]{2,0,1:T(8,128)} %get-tuple-element.48) | copy-start | bytes 2752516
  85.1 1.2 copy-start.1
  87.6 1.0 copy-start.8
  88.4 1.1 copy-start.2
  90.6 56.8 %all-to-all-start = ((f32[128,1,2304]{2,1,0:T(1,128)}), f32[128,1,2304]{2,1,0:T(1,128)S(1)}, u32[]{:S(2)}, u32[]{:S(2)}) async-start(f32[128,1,2304]{2,1,0:T(1,128)} %bitcast.393), calls=%async_computation | async-start | bytes 2359296 | tf_op jit(solution)/shard_map/all_to_all | solution.py:178
  149.8 39.0 %all-to-all-start.1 = ((f32[128,1,2304]{2,1,0:T(1,128)}), f32[128,1,2304]{2,1,0:T(1,128)S(1)}, u32[]{:S(2)}, u32[]{:S(2)}) async-start(f32[128,1,2304]{2,1,0:T(1,128)} %broadcast_in_dim.2), calls=%async_computation.1 | async-start | bytes 2359296 | tf_op jit(solution)/shard_map/all_to_all | solution.py:181
  158.4 7.4 %collective-permute-start.5 = (bf16[64,1,512]{2,0,1:T(8,128)(2,1)S(1)}, bf16[64,1,512]{2,0,1:T(8,128)(2,1)S(1)}, u32[]{:S(2)}, u32[]{:S(2)}) collective-permute-start(bf16[64,1,512]{2,0,1:T(8,128)(2,1)S(1)} %get-tuple-element.38), channel_id=1, source_target_pairs={{0,2},{2,4},{4,6},{6,8},{8,10},{10,12},{12,14},{14,16},{16,18},{18... | collective-permute-start | bytes 196616 | tf_op jit(solution)/shard_map/ppermute | solution.py:24
  159.9 5.9 %collective-permute-start.6 = (bf16[64,1,512]{2,0,1:T(8,128)(2,1)S(1)}, bf16[64,1,512]{2,0,1:T(8,128)(2,1)S(1)}, u32[]{:S(2)}, u32[]{:S(2)}) collective-permute-start(bf16[64,1,512]{2,0,1:T(8,128)(2,1)S(1)} %get-tuple-element.39), channel_id=1, source_target_pairs={{0,254},{2,0},{4,2},{6,4},{8,6},{10,8},{12,10},{14,12},{16,14},{18... | collective-permute-start | bytes 196616 | tf_op jit(solution)/shard_map/ppermute | solution.py:24
Sparse Core Ops, SparseCore 0:
  17.2 16.2 all-gather.2

commit v4 on v2

--- a/solution.py
+++ b/solution.py
@@ -164,18 +164,18 @@
     return (source == wanted).astype(jnp.bfloat16)
 
 
-def summed_over_cycle(parts, axis):
+def summed_over_cycle(parts, axis, finished):
     devices = lax.axis_size(axis)
     flat = jnp.concatenate([p.reshape(-1) for p in parts])
     pieces = lax.all_to_all(flat.reshape(devices, -1), axis, 0, 0, tiled=True)
-    total = jnp.sum(pieces, axis=0)
+    total, finished = lax.optimization_barrier((jnp.sum(pieces, axis=0), finished))
     spread = jnp.broadcast_to(total[None], (devices,) + total.shape)
     whole = lax.all_to_all(spread, axis, 0, 0, tiled=True).reshape(-1)
     out, start = [], 0
     for p in parts:
         out.append(whole[start : start + p.size].reshape(p.shape))
         start += p.size
-    return out
+    return out, finished
 
 
 def gelu_back(pre_act, grad_in):
@@ -230,7 +230,7 @@
     first_delta = gelu_back(first_pre, first_back).astype(jnp.bfloat16)
     first_grad = weight_taps(first_delta, first_pad)
     input_back = input_grad(first_delta, own_inputs(w_first)).astype(jnp.bfloat16)
-    reduced = summed_over_cycle((first_grad, second_grad, third_grad), "blk")
+    reduced, input_back = summed_over_cycle((first_grad, second_grad, third_grad), "blk", input_back)
     cell_count = inputs.shape[1] * inputs.shape[2] * lax.axis_size("blk")
     return (
         orient(input_back, mirrored),

time: 166 us -> 172 us (1.036)
  waiting for transfers between devices: 53.8 us -> 60.1 us
    all_to_all x1, waiting for transfers between devices: 21.4 us -> 31.8 us  [summed_over_cycle(): whole = lax.all_to_all(spread, axis, 0, 0, tiled=True).reshape(-1)]
    all_to_all x1, waiting for transfers between devices: 27.3 us -> 23.4 us  [summed_over_cycle(): pieces = lax.all_to_all(flat.reshape(devices, -1), axis, 0, 0, tiled=True)]
    unnamed x19 -> x31, local copies, waits for them, and re-layouts: 4.46 us -> 4.85 us
where the time goes in v4:
time: 172 us; the launch traced here: 171 us
  waiting for transfers between devices  60.1 us (35%)
  starting transfers between devices  41.4 us (24%)
  matrix products  25.6 us (15%)
  blocking collectives  19.8 us (12%)
  local copies, waits for them, and re-layouts  16 us (9%)
  other arithmetic  6.4 us (4%)
  between operations  2.12 us (1%)
    all_to_all x1, waiting for transfers between devices, summed_over_cycle(): whole = lax.all_to_all(spread, axis, 0, 0, tiled=True).reshape(-1)  31.8 us
    all_to_all x1, waiting for transfers between devices, summed_over_cycle(): pieces = lax.all_to_all(flat.reshape(devices, -1), axis, 0, 0, tiled=True)  23.4 us
    all_to_all x1, starting transfers between devices, summed_over_cycle(): pieces = lax.all_to_all(flat.reshape(devices, -1), axis, 0, 0, tiled=True)  21.7 us
    ppermute x5, starting transfers between devices, passed_along(): lax.ppermute(shard, axis, [(i, (i + by) % devices) for i in range(devices)])  9.04 us
    dot_general x18, matrix products, weight_taps(): jnp.einsum('orw,irw->oi', grad_out, framed[:, row_tap:row_tap + row_count...  7.22 us
    dot_general x18, matrix products, conv_taps(): jnp.einsum('oi,irw->orw', weight[row_tap, col_tap], framed[:, row_tap:row...  7.17 us
    dot_general x18, matrix products, spread_taps(): jnp.einsum('oi,orw->irw', weight[row_tap, col_tap], framed[:, row_start:r...  7.11 us
    all_to_all x1, starting transfers between devices, summed_over_cycle(): whole = lax.all_to_all(spread, axis, 0, 0, tiled=True).reshape(-1)  6.49 us
  transfers between devices with their start and end apart: 9, of which 4 were waited for; matrix products, arithmetic and copies ran while one was open for 10% of the time, Pallas kernels for 0%

profile of v4, /device:TPU:8, one launch (start us, length us, event | category | flops | bytes accessed | tf_op | source)
XLA Modules:
  0.0 171.5 jit_solution(4567074501963515020)
XLA Ops:
  2.9 2.3 %all_gather.30 = bf16[128,4,512]{2,0,1:T(8,128)(2,1)S(1)} all-gather(bf16[64,4,512]{2,0,1:T(8,128)(2,1)S(1)} %broadcast_select_fusion.1), channel_id=1, replica_groups=mesh['blk'=128,'chan'=2] {'chan'}, dimensions={0}, use_global_device_ids=true | all-gather | bytes 786432 | tf_op jit(solution)/shard_map/all_gather | solution.py:37
  6.0 1.5 collective-permute-start.1
  8.3 2.6 %collective-permute-start.2 = (bf16[128,2,512]{2,0,1:T(8,128)(2,1)}, bf16[128,2,512]{2,0,1:T(8,128)(2,1)}, u32[]{:S(2)}, u32[]{:S(2)}) collective-permute-start(bf16[128,2,512]{2,0,1:T(8,128)(2,1)} %slice.570), channel_id=1, source_target_pairs={{2,0},{4,2},{6,4},{8,6},{10,8},{12,10},{14,12},{16,14},{18,16},{20... | collective-permute-start | bytes 786440 | tf_op jit(solution)/shard_map/ppermute | solution.py:42
  11.2 2.0 %all_gather.29 = bf16[256,2,256]{0,2,1:T(8,128)(2,1)S(1)} all-gather(bf16[128,2,256]{0,2,1:T(8,128)(2,1)S(1)} %broadcast_select_fusion.2), channel_id=1, replica_groups=mesh['blk'=128,'chan'=2] {'chan'}, dimensions={0}, use_global_device_ids=true | all-gather | bytes 393216 | tf_op jit(solution)/shard_map/all_gather | solution.py:156
  13.5 2.2 %all_gather.28 = bf16[3,3,256,128]{2,3,1,0:T(8,128)(2,1)S(1)} all-gather(bf16[3,3,128,128]{2,3,1,0:T(8,128)(2,1)S(1)} %copy.61), channel_id=1, replica_groups=mesh['blk'=128,'chan'=2] {'chan'}, dimensions={2}, use_global_device_ids=true | all-gather | bytes 884736 | tf_op jit(solution)/shard_map/all_gather | solution.py:145
  19.2 2.3 %reshape.57 = f32[64,6,514]{0,2,1:T(8,128)} reshape(f32[64,3,2,257,2]{0,4,3,2,1:T(2,128)S(1)} %copy.64) | data formatting | bytes 1579008 | tf_op jit(solution)/shard_map/reshape | solution.py:127
  26.0 2.0 %all_gather.27 = bf16[3,3,128,128]{3,2,1,0:T(8,128)(2,1)S(1)} all-gather(bf16[3,3,64,128]{3,2,1,0:T(8,128)(2,1)S(1)} %copy-done.3), channel_id=1, replica_groups=mesh['blk'=128,'chan'=2] {'chan'}, dimensions={2}, use_global_device_ids=true | all-gather | bytes 442368 | tf_op jit(solution)/shard_map/all_gather | solution.py:145
  28.0 2.0 %all_gather.34 = bf16[3,3,128,128]{3,2,1,0:T(8,128)(2,1)S(1)} all-gather(bf16[3,3,64,128]{3,2,1,0:T(8,128)(2,1)S(1)} %copy-done.2), channel_id=1, replica_groups=mesh['blk'=128,'chan'=2] {'chan'}, dimensions={2}, use_global_device_ids=true | all-gather | bytes 442368 | tf_op jit(solution)/shard_map/all_gather | solution.py:145
  36.2 2.6 %all_gather.31 = bf16[128,7,512]{2,0,1:T(8,128)(2,1)S(1)} all-gather(bf16[64,7,512]{2,0,1:T(8,128)(2,1)S(1)} %get-tuple-element.45), channel_id=1, replica_groups=mesh['blk'=128,'chan'=2] {'chan'}, dimensions={0}, use_global_device_ids=true | all-gather | bytes 1376256 | tf_op jit(solution)/shard_map/all_gather | solution.py:194
  42.1 2.3 %all_gather.33 = bf16[128,5,512]{2,0,1:T(8,128)(2,1)S(1)} all-gather(bf16[64,5,512]{2,0,1:T(8,128)(2,1)S(1)} %get-tuple-element.47), channel_id=1, replica_groups=mesh['blk'=128,'chan'=2] {'chan'}, dimensions={0}, use_global_device_ids=true | all-gather | bytes 983040 | tf_op jit(solution)/shard_map/all_gather | solution.py:199
  50.5 2.2 %all_gather.32 = bf16[128,4,512]{2,0,1:T(8,128)(2,1)S(1)} all-gather(bf16[64,4,512]{2,0,1:T(8,128)(2,1)S(1)} %fusion.63), channel_id=1, replica_groups=mesh['blk'=128,'chan'=2] {'chan'}, dimensions={0}, use_global_device_ids=true | all-gather | bytes 786432 | tf_op jit(solution)/shard_map/all_gather | solution.py:151
  56.5 1.6 collective-permute-start.3
  58.1 2.6 %collective-permute-start.4 = (bf16[64,1,512]{2,0,1:T(8,128)(2,1)S(1)}, bf16[64,1,512]{2,0,1:T(8,128)(2,1)S(1)}, u32[]{:S(2)}, u32[]{:S(2)}) collective-permute-start(bf16[64,1,512]{2,0,1:T(8,128)(2,1)S(1)} %get-tuple-element.39), channel_id=1, source_target_pairs={{0,254},{2,0},{4,2},{6,4},{8,6},{10,8},{12,10},{14,12},{16,14},{18... | collective-permute-start | bytes 196616 | tf_op jit(solution)/shard_map/ppermute | solution.py:24
  60.8 2.1 %collective-permute-done.3 = bf16[64,1,512]{2,0,1:T(8,128)(2,1)S(1)} collective-permute-done((bf16[64,1,512]{2,0,1:T(8,128)(2,1)S(1)}, bf16[64,1,512]{2,0,1:T(8,128)(2,1)S(1)}, u32[]{:S(2)}, u32[]{:S(2)}) %collective-permute-start.3) | collective-permute-done | bytes 65568 | tf_op jit(solution)/shard_map/ppermute | solution.py:24
  66.3 2.2 %all_gather.35 = bf16[128,4,512]{2,0,1:T(8,128)(2,1)S(1)} all-gather(bf16[64,4,512]{2,0,1:T(8,128)(2,1)S(1)} %fusion.70), channel_id=1, replica_groups=mesh['blk'=128,'chan'=2] {'chan'}, dimensions={0}, use_global_device_ids=true | all-gather | bytes 786432 | tf_op jit(solution)/shard_map/all_gather | solution.py:151
  70.8 21.7 %all-to-all-start = ((f32[128,1,2304]{2,1,0:T(1,128)}), f32[128,1,2304]{2,1,0:T(1,128)S(1)}, u32[]{:S(2)}, u32[]{:S(2)}) async-start(f32[128,1,2304]{2,1,0:T(1,128)} %bitcast.144), calls=%async_computation | async-start | bytes 2359296 | tf_op jit(solution)/shard_map/all_to_all | solution.py:170
  96.2 1.5 collective-permute-start.5
  97.7 2.7 %collective-permute-start.6 = (bf16[64,1,512]{2,0,1:T(8,128)(2,1)S(1)}, bf16[64,1,512]{2,0,1:T(8,128)(2,1)S(1)}, u32[]{:S(2)}, u32[]{:S(2)}) collective-permute-start(bf16[64,1,512]{2,0,1:T(8,128)(2,1)S(1)} %get-tuple-element.37), channel_id=1, source_target_pairs={{0,254},{2,0},{4,2},{6,4},{8,6},{10,8},{12,10},{14,12},{16,14},{18... | collective-permute-start | bytes 196616 | tf_op jit(solution)/shard_map/ppermute | solution.py:24
  100.4 2.8 %collective-permute-done.5 = bf16[64,1,512]{2,0,1:T(8,128)(2,1)S(1)} collective-permute-done((bf16[64,1,512]{2,0,1:T(8,128)(2,1)S(1)}, bf16[64,1,512]{2,0,1:T(8,128)(2,1)S(1)}, u32[]{:S(2)}, u32[]{:S(2)}) %collective-permute-start.5) | collective-permute-done | bytes 65568 | tf_op jit(solution)/shard_map/ppermute | solution.py:24
  103.3 23.4 %all-to-all-done = f32[128,1,2304]{2,1,0:T(1,128)S(1)} async-done(((f32[128,1,2304]{2,1,0:T(1,128)}), f32[128,1,2304]{2,1,0:T(1,128)S(1)}, u32[]{:S(2)}, u32[]{:S(2)}) %all-to-all-start) | async-done | bytes 1179680 | tf_op jit(solution)/shard_map/all_to_all | solution.py:170
  127.4 1.6 broadcast_in_dim.2
  129.0 6.5 %all-to-all-start.1 = ((f32[128,1,2304]{2,1,0:T(1,128)}), f32[128,1,2304]{2,1,0:T(1,128)S(1)}, u32[]{:S(2)}, u32[]{:S(2)}) async-start(f32[128,1,2304]{2,1,0:T(1,128)} %broadcast_in_dim.2), calls=%async_computation.1 | async-start | bytes 2359296 | tf_op jit(solution)/shard_map/all_to_all | solution.py:173
  137.0 31.8 %all-to-all-done.1 = f32[128,1,2304]{2,1,0:T(1,128)S(1)} async-done(((f32[128,1,2304]{2,1,0:T(1,128)}), f32[128,1,2304]{2,1,0:T(1,128)S(1)}, u32[]{:S(2)}, u32[]{:S(2)}) %all-to-all-start.1) | async-done | bytes 1179680 | tf_op jit(solution)/shard_map/all_to_all | solution.py:173
  168.8 1.4 slice_multiply_fusion.1
  (150 shorter events, 43.4 us)
Async XLA Ops:
  0.6 2.2 %copy-start.1 = (bf16[64,4,512]{2,1,0:T(4,128)(2,1)S(1)}, bf16[64,4,512]{2,1,0:T(4,128)(2,1)}, u32[]{:S(2)}) copy-start(bf16[64,4,512]{2,1,0:T(4,128)(2,1)} %param.6) | copy-start | bytes 786436
  2.9 8.0 %copy-start.8 = (bf16[128,2,256]{2,1,0:T(2,128)(2,1)S(1)}, bf16[128,2,256]{2,1,0:T(2,128)(2,1)}, u32[]{:S(2)}) copy-start(bf16[128,2,256]{2,1,0:T(2,128)(2,1)} %param.10) | copy-start | bytes 393220
  5.3 8.0 %copy-start.7 = (bf16[3,3,128,128]{3,2,1,0:T(8,128)(2,1)S(1)}, bf16[3,3,128,128]{3,2,1,0:T(8,128)(2,1)}, u32[]{:S(2)}) copy-start(bf16[3,3,128,128]{3,2,1,0:T(8,128)(2,1)} %param.9) | copy-start | bytes 884740
  6.0 24.0 %collective-permute-start.1 = (bf16[128,3,512]{2,0,1:T(8,128)(2,1)}, bf16[128,3,512]{2,0,1:T(8,128)(2,1)}, u32[]{:S(2)}, u32[]{:S(2)}) collective-permute-start(bf16[128,3,512]{2,0,1:T(8,128)(2,1)} %slice.569), channel_id=1, source_target_pairs={{0,2},{2,4},{4,6},{6,8},{8,10},{10,12},{12,14},{14,16},{16,18},{18... | collective-permute-start | bytes 1179656 | tf_op jit(solution)/shard_map/ppermute | solution.py:41
  8.3 23.0 %collective-permute-start.2 = (bf16[128,2,512]{2,0,1:T(8,128)(2,1)}, bf16[128,2,512]{2,0,1:T(8,128)(2,1)}, u32[]{:S(2)}, u32[]{:S(2)}) collective-permute-start(bf16[128,2,512]{2,0,1:T(8,128)(2,1)} %slice.570), channel_id=1, source_target_pairs={{2,0},{4,2},{6,4},{8,6},{10,8},{12,10},{14,12},{16,14},{18,16},{20... | collective-permute-start | bytes 786440 | tf_op jit(solution)/shard_map/ppermute | solution.py:42
  21.5 3.6 %copy-start = (f32[64,6,514]{0,2,1:T(8,128)S(1)}, f32[64,6,514]{0,2,1:T(8,128)}, u32[]{:S(2)}) copy-start(f32[64,6,514]{0,2,1:T(8,128)} %reshape.57) | copy-start | bytes 2368516
  22.7 7.3 %collective-permute-start = (bf16[64,1,512]{2,0,1:T(8,128)(2,1)S(1)}, bf16[64,1,512]{2,0,1:T(8,128)(2,1)S(1)}, u32[]{:S(2)}, u32[]{:S(2)}) collective-permute-start(bf16[64,1,512]{2,0,1:T(8,128)(2,1)S(1)} %copy.102), channel_id=1, source_target_pairs={{0,254},{2,0},{4,2},{6,4},{8,6},{10,8},{12,10},{14,12},{16,14},{18... | collective-permute-start | bytes 196616 | tf_op jit(solution)/shard_map/ppermute | solution.py:24
  25.1 0.9 copy-start.3
  25.2 2.8 %copy-start.2 = (bf16[3,3,64,128]{3,2,1,0:T(8,128)(2,1)S(1)}, bf16[3,3,64,128]{3,2,1,0:T(8,128)(2,1)}, u32[]{:S(2)}) copy-start(bf16[3,3,64,128]{3,2,1,0:T(8,128)(2,1)} %param.7) | copy-start | bytes 442372
  41.6 2.8 %copy-start.9 = (s32[768]{0:T(1024)S(1)}, s32[768]{0:T(1024)}, u32[]{:S(2)}) copy-start(s32[768]{0:T(1024)} %get-tuple-element.57) | copy-start | bytes 9220
  41.6 2.8 %copy-start.10 = (s32[768]{0:T(1024)S(1)}, s32[768]{0:T(1024)}, u32[]{:S(2)}) copy-start(s32[768]{0:T(1024)} %get-tuple-element.58) | copy-start | bytes 9220
  44.4 1.0 copy-start.4
  44.4 1.1 copy-start.5
  44.4 1.2 copy-start.6
  56.5 6.5 %collective-permute-start.3 = (bf16[64,1,512]{2,0,1:T(8,128)(2,1)S(1)}, bf16[64,1,512]{2,0,1:T(8,128)(2,1)S(1)}, u32[]{:S(2)}, u32[]{:S(2)}) collective-permute-start(bf16[64,1,512]{2,0,1:T(8,128)(2,1)S(1)} %get-tuple-element.38), channel_id=1, source_target_pairs={{0,2},{2,4},{4,6},{6,8},{8,10},{10,12},{12,14},{14,16},{16,18},{18... | collective-permute-start | bytes 196616 | tf_op jit(solution)/shard_map/ppermute | solution.py:24
  58.1 4.9 %collective-permute-start.4 = (bf16[64,1,512]{2,0,1:T(8,128)(2,1)S(1)}, bf16[64,1,512]{2,0,1:T(8,128)(2,1)S(1)}, u32[]{:S(2)}, u32[]{:S(2)}) collective-permute-start(bf16[64,1,512]{2,0,1:T(8,128)(2,1)S(1)} %get-tuple-element.39), channel_id=1, source_target_pairs={{0,254},{2,0},{4,2},{6,4},{8,6},{10,8},{12,10},{14,12},{16,14},{18... | collective-permute-start | bytes 196616 | tf_op jit(solution)/shard_map/ppermute | solution.py:24
  70.8 55.8 %all-to-all-start = ((f32[128,1,2304]{2,1,0:T(1,128)}), f32[128,1,2304]{2,1,0:T(1,128)S(1)}, u32[]{:S(2)}, u32[]{:S(2)}) async-start(f32[128,1,2304]{2,1,0:T(1,128)} %bitcast.144), calls=%async_computation | async-start | bytes 2359296 | tf_op jit(solution)/shard_map/all_to_all | solution.py:170
  96.2 7.0 %collective-permute-start.5 = (bf16[64,1,512]{2,0,1:T(8,128)(2,1)S(1)}, bf16[64,1,512]{2,0,1:T(8,128)(2,1)S(1)}, u32[]{:S(2)}, u32[]{:S(2)}) collective-permute-start(bf16[64,1,512]{2,0,1:T(8,128)(2,1)S(1)} %get-tuple-element.36), channel_id=1, source_target_pairs={{0,2},{2,4},{4,6},{6,8},{8,10},{10,12},{12,14},{14,16},{16,18},{18... | collective-permute-start | bytes 196616 | tf_op jit(solution)/shard_map/ppermute | solution.py:24
  97.7 5.5 %collective-permute-start.6 = (bf16[64,1,512]{2,0,1:T(8,128)(2,1)S(1)}, bf16[64,1,512]{2,0,1:T(8,128)(2,1)S(1)}, u32[]{:S(2)}, u32[]{:S(2)}) collective-permute-start(bf16[64,1,512]{2,0,1:T(8,128)(2,1)S(1)} %get-tuple-element.37), channel_id=1, source_target_pairs={{0,254},{2,0},{4,2},{6,4},{8,6},{10,8},{12,10},{14,12},{16,14},{18... | collective-permute-start | bytes 196616 | tf_op jit(solution)/shard_map/ppermute | solution.py:24
  129.0 39.8 %all-to-all-start.1 = ((f32[128,1,2304]{2,1,0:T(1,128)}), f32[128,1,2304]{2,1,0:T(1,128)S(1)}, u32[]{:S(2)}, u32[]{:S(2)}) async-start(f32[128,1,2304]{2,1,0:T(1,128)} %broadcast_in_dim.2), calls=%async_computation.1 | async-start | bytes 2359296 | tf_op jit(solution)/shard_map/all_to_all | solution.py:173

commit v5 on v3

--- a/solution.py
+++ b/solution.py
@@ -142,15 +142,14 @@
 
 
 def own_inputs(weights):
-    sizes = [w.shape[2] for w in weights]
     devices = lax.axis_size("chan")
-    whole = lax.all_gather(jnp.concatenate(weights, axis=2), "chan", axis=0, tiled=False)
-    width = weights[0].shape[3] // devices
-    mine = lax.dynamic_slice_in_dim(whole, lax.axis_index("chan") * width, width, axis=4)
+    blocks = jnp.concatenate(weights, axis=2)
+    blocks = blocks.reshape(blocks.shape[:3] + (devices, blocks.shape[3] // devices))
+    swapped = lax.all_to_all(jnp.moveaxis(blocks, 3, 0), "chan", 0, 0, tiled=False)
     out, start = [], 0
-    for size in sizes:
-        parts = [mine[d, :, :, start : start + size] for d in range(devices)]
-        out.append(jnp.concatenate(parts, axis=2))
+    for w in weights:
+        size = w.shape[2]
+        out.append(jnp.concatenate([swapped[d, :, :, start : start + size] for d in range(devices)], axis=2))
         start += size
     return out
 
@@ -231,7 +230,8 @@
         ],
         axis=1,
     )
-    first_mine, second_mine, third_mine = own_inputs((w_first, w_second, w_third))
+    (third_mine,) = own_inputs((w_third,))
+    first_mine, second_mine = own_inputs((w_first, w_second))
     second_back = third_input_grad(upstream, third_mine)
     second_delta = gelu_back(second_pre, second_back).astype(jnp.bfloat16)
     second_grad = weight_taps(second_delta, second_pad)

time: 199 us -> 176 us (0.88)
  between operations: 15.6 us -> 2.18 us
  waiting for transfers between devices: 64.5 us -> 56.8 us
  local copies, waits for them, and re-layouts: 27.2 us -> 21.3 us
  starting transfers between devices: 43.6 us -> 48 us
    all_to_all x0 -> x2, starting transfers between devices: none -> 6.9 us  [own_inputs(): lax.all_to_all(jnp.moveaxis(blocks, 3, 0), 'chan', 0, 0, tiled=False)]
    ppermute x1, waiting for transfers between devices: 5.53 us -> 0.01 us  [widen_by(): before = lax.ppermute(gathered[:, length - before_rows:], 'blk', up)]
    ppermute x5, waiting for transfers between devices: 7.72 us -> 5.31 us  [passed_along(): lax.ppermute(shard, axis, [(i, (i + by) % devices) for i in range(devices)])]
    all_gather x1 -> x0, local copies, waits for them, and re-layouts: 2.38 us -> none  [own_inputs(): lax.all_gather(jnp.concatenate(weights, axis=2), 'chan', axis=0, tiled=Fa...]
    all_to_all x1, starting transfers between devices: 23.8 us -> 21.6 us  [summed_over_cycle(): pieces = lax.all_to_all(flat.reshape(devices, -1), axis, 0, 0, tiled=True)]
    squeeze x2, local copies, waits for them, and re-layouts: 2.32 us -> 0.17 us  [own_inputs(): swapped[d, :, :, start:start + size]]
    slice x1, local copies, waits for them, and re-layouts: 2.1 us -> 0.05 us  [fold_rims(): interior[:, :-1]]
    unnamed x34 -> x35, local copies, waits for them, and re-layouts: 6.88 us -> 6.32 us
  transfers between devices with their start and end apart: 10 -> 11, of which waited for: 6 -> 5; matrix products, arithmetic and copies ran while one was open for 10% -> 13% of each run, Pallas kernels for 0% -> 0%
where the time goes in v5:
time: 176 us; the launch traced here: 175 us
  waiting for transfers between devices  56.8 us (32%)
  starting transfers between devices  48 us (27%)
  matrix products  25.2 us (14%)
  local copies, waits for them, and re-layouts  21.3 us (12%)
  blocking collectives  14 us (8%)
  other arithmetic  7.87 us (4%)
  between operations  2.18 us (1%)
    all_to_all x1, waiting for transfers between devices, summed_over_cycle(): pieces = lax.all_to_all(flat.reshape(devices, -1), axis, 0, 0, tiled=True)  29.6 us
    all_to_all x1, starting transfers between devices, summed_over_cycle(): pieces = lax.all_to_all(flat.reshape(devices, -1), axis, 0, 0, tiled=True)  21.6 us
    all_to_all x1, waiting for transfers between devices, summed_over_cycle(): whole = lax.all_to_all(spread, axis, 0, 0, tiled=True).reshape(-1)  21.5 us
    ppermute x5, starting transfers between devices, passed_along(): lax.ppermute(shard, axis, [(i, (i + by) % devices) for i in range(devices)])  8.99 us
    dot_general x18, matrix products, weight_taps(): jnp.einsum('orw,irw->oi', grad_out, framed[:, row_tap:row_tap + row_count...  7.29 us
    dot_general x18, matrix products, conv_taps(): jnp.einsum('oi,irw->orw', weight[row_tap, col_tap], framed[:, row_tap:row...  7.16 us
    all_to_all x2, starting transfers between devices, own_inputs(): lax.all_to_all(jnp.moveaxis(blocks, 3, 0), 'chan', 0, 0, tiled=False)  6.9 us
    dot_general x18, matrix products, spread_taps(): jnp.einsum('oi,orw->irw', weight[row_tap, col_tap], framed[:, row_start:r...  6.59 us
  transfers between devices with their start and end apart: 11, of which 5 were waited for; matrix products, arithmetic and copies ran while one was open for 13% of the time, Pallas kernels for 0%

profile of v5, /device:TPU:8, one launch (start us, length us, event | category | flops | bytes accessed | tf_op | source)
XLA Modules:
  0.0 175.2 jit_solution(14028860764118627777)
XLA Ops:
  2.9 2.3 %all_gather.19 = bf16[128,4,512]{2,0,1:T(8,128)(2,1)S(1)} all-gather(bf16[64,4,512]{2,0,1:T(8,128)(2,1)S(1)} %broadcast_select_fusion.1), channel_id=1, replica_groups=mesh['blk'=128,'chan'=2] {'chan'}, dimensions={0}, use_global_device_ids=true | all-gather | bytes 786432 | tf_op jit(solution)/shard_map/all_gather | solution.py:37
  6.0 1.5 collective-permute-start.1
  8.2 2.6 %collective-permute-start.2 = (bf16[128,2,512]{2,0,1:T(8,128)(2,1)}, bf16[128,2,512]{2,0,1:T(8,128)(2,1)}, u32[]{:S(2)}, u32[]{:S(2)}) collective-permute-start(bf16[128,2,512]{2,0,1:T(8,128)(2,1)} %slice.620), channel_id=1, source_target_pairs={{2,0},{4,2},{6,4},{8,6},{10,8},{12,10},{14,12},{16,14},{18,16},{20... | collective-permute-start | bytes 786440 | tf_op jit(solution)/shard_map/ppermute | solution.py:42
  11.8 3.4 %all-to-all-start.1 = ((bf16[2,3,3,128,64]{3,4,2,1,0:T(8,128)(2,1)}), bf16[2,3,3,128,64]{3,4,2,1,0:T(8,128)(2,1)S(1)}, u32[]{:S(2)}, u32[]{:S(2)}) async-start(bf16[2,3,3,128,64]{3,4,2,1,0:T(8,128)(2,1)} %bitcast.398), calls=%async_computation.1 | async-start | bytes 589824 | tf_op jit(solution)/shard_map/all_to_all | solution.py:148
  15.6 2.1 %all_gather.18 = bf16[256,2,256]{0,2,1:T(8,128)(2,1)S(1)} all-gather(bf16[128,2,256]{0,2,1:T(8,128)(2,1)S(1)} %broadcast_select_fusion.2), channel_id=1, replica_groups=mesh['blk'=128,'chan'=2] {'chan'}, dimensions={0}, use_global_device_ids=true | all-gather | bytes 393216 | tf_op jit(solution)/shard_map/all_gather | solution.py:163
  21.2 2.7 %copy.70 = f32[64,3,2,257,2]{0,4,3,2,1:T(2,128)S(1)} copy(f32[64,3,2,257,2]{3,0,1,4,2:T(8,128)} %pad_maximum_fusion) | data formatting | bytes 1579008 | tf_op jit(solution)/shard_map/stack | solution.py:126
  23.9 2.3 %reshape.65 = f32[64,6,514]{0,2,1:T(8,128)} reshape(f32[64,3,2,257,2]{0,4,3,2,1:T(2,128)S(1)} %copy.70) | data formatting | bytes 1579008 | tf_op jit(solution)/shard_map/reshape | solution.py:127
  29.8 3.4 %all-to-all-start = ((bf16[2,3,3,128,64]{3,4,2,1,0:T(8,128)(2,1)}), bf16[2,3,3,128,64]{3,4,2,1,0:T(8,128)(2,1)S(1)}, u32[]{:S(2)}, u32[]{:S(2)}) async-start(bf16[2,3,3,128,64]{3,4,2,1,0:T(8,128)(2,1)} %bitcast.399), calls=%async_computation | async-start | bytes 589824 | tf_op jit(solution)/shard_map/all_to_all | solution.py:148
  44.2 2.9 %all_gather.20 = bf16[128,7,512]{2,0,1:T(8,128)(2,1)S(1)} all-gather(bf16[64,7,512]{2,0,1:T(8,128)(2,1)S(1)} %get-tuple-element.47), channel_id=1, replica_groups=mesh['blk'=128,'chan'=2] {'chan'}, dimensions={0}, use_global_device_ids=true | all-gather | bytes 1376256 | tf_op jit(solution)/shard_map/all_gather | solution.py:201
  50.8 2.2 %all_gather.21 = bf16[128,4,512]{2,0,1:T(8,128)(2,1)S(1)} all-gather(bf16[64,4,512]{2,0,1:T(8,128)(2,1)S(1)} %fusion.63), channel_id=1, replica_groups=mesh['blk'=128,'chan'=2] {'chan'}, dimensions={0}, use_global_device_ids=true | all-gather | bytes 786432 | tf_op jit(solution)/shard_map/all_gather | solution.py:158
  56.2 2.3 %all_gather.23 = bf16[128,5,512]{2,0,1:T(8,128)(2,1)S(1)} all-gather(bf16[64,5,512]{2,0,1:T(8,128)(2,1)S(1)} %get-tuple-element.53), channel_id=1, replica_groups=mesh['blk'=128,'chan'=2] {'chan'}, dimensions={0}, use_global_device_ids=true | all-gather | bytes 983040 | tf_op jit(solution)/shard_map/all_gather | solution.py:206
  64.3 1.6 collective-permute-start.3
  65.9 2.6 %collective-permute-start.4 = (bf16[64,1,512]{2,0,1:T(8,128)(2,1)S(1)}, bf16[64,1,512]{2,0,1:T(8,128)(2,1)S(1)}, u32[]{:S(2)}, u32[]{:S(2)}) collective-permute-start(bf16[64,1,512]{2,0,1:T(8,128)(2,1)S(1)} %get-tuple-element.35), channel_id=1, source_target_pairs={{0,254},{2,0},{4,2},{6,4},{8,6},{10,8},{12,10},{14,12},{16,14},{18... | collective-permute-start | bytes 196616 | tf_op jit(solution)/shard_map/ppermute | solution.py:24
  68.7 2.1 %collective-permute-done.3 = bf16[64,1,512]{2,0,1:T(8,128)(2,1)S(1)} collective-permute-done((bf16[64,1,512]{2,0,1:T(8,128)(2,1)S(1)}, bf16[64,1,512]{2,0,1:T(8,128)(2,1)S(1)}, u32[]{:S(2)}, u32[]{:S(2)}) %collective-permute-start.3) | collective-permute-done | bytes 65568 | tf_op jit(solution)/shard_map/ppermute | solution.py:24
  76.6 21.6 %all-to-all-start.2 = ((f32[128,1,2304]{2,1,0:T(1,128)}), f32[128,1,2304]{2,1,0:T(1,128)S(1)}, u32[]{:S(2)}, u32[]{:S(2)}) async-start(f32[128,1,2304]{2,1,0:T(1,128)} %bitcast.172), calls=%async_computation.2 | async-start | bytes 2359296 | tf_op jit(solution)/shard_map/all_to_all | solution.py:177
  98.2 2.2 %all_gather.22 = bf16[128,4,512]{2,0,1:T(8,128)(2,1)S(1)} all-gather(bf16[64,4,512]{2,0,1:T(8,128)(2,1)S(1)} %fusion.70), channel_id=1, replica_groups=mesh['blk'=128,'chan'=2] {'chan'}, dimensions={0}, use_global_device_ids=true | all-gather | bytes 786432 | tf_op jit(solution)/shard_map/all_gather | solution.py:158
  101.5 29.6 %all-to-all-done.2 = f32[128,1,2304]{2,1,0:T(1,128)S(1)} async-done(((f32[128,1,2304]{2,1,0:T(1,128)}), f32[128,1,2304]{2,1,0:T(1,128)S(1)}, u32[]{:S(2)}, u32[]{:S(2)}) %all-to-all-start.2) | async-done | bytes 1179680 | tf_op jit(solution)/shard_map/all_to_all | solution.py:177
  131.8 1.6 broadcast_in_dim.2
  133.5 6.3 %all-to-all-start.3 = ((f32[128,1,2304]{2,1,0:T(1,128)}), f32[128,1,2304]{2,1,0:T(1,128)S(1)}, u32[]{:S(2)}, u32[]{:S(2)}) async-start(f32[128,1,2304]{2,1,0:T(1,128)} %broadcast_in_dim.2), calls=%async_computation.3 | async-start | bytes 2359296 | tf_op jit(solution)/shard_map/all_to_all | solution.py:180
  142.1 1.5 collective-permute-start.5
  143.6 2.7 %collective-permute-start.6 = (bf16[64,1,512]{2,0,1:T(8,128)(2,1)S(1)}, bf16[64,1,512]{2,0,1:T(8,128)(2,1)S(1)}, u32[]{:S(2)}, u32[]{:S(2)}) collective-permute-start(bf16[64,1,512]{2,0,1:T(8,128)(2,1)S(1)} %get-tuple-element.33), channel_id=1, source_target_pairs={{0,254},{2,0},{4,2},{6,4},{8,6},{10,8},{12,10},{14,12},{16,14},{18... | collective-permute-start | bytes 196616 | tf_op jit(solution)/shard_map/ppermute | solution.py:24
  146.3 3.2 %collective-permute-done.5 = bf16[64,1,512]{2,0,1:T(8,128)(2,1)S(1)} collective-permute-done((bf16[64,1,512]{2,0,1:T(8,128)(2,1)S(1)}, bf16[64,1,512]{2,0,1:T(8,128)(2,1)S(1)}, u32[]{:S(2)}, u32[]{:S(2)}) %collective-permute-start.5) | collective-permute-done | bytes 65568 | tf_op jit(solution)/shard_map/ppermute | solution.py:24
  151.0 21.5 %all-to-all-done.3 = f32[128,1,2304]{2,1,0:T(1,128)S(1)} async-done(((f32[128,1,2304]{2,1,0:T(1,128)}), f32[128,1,2304]{2,1,0:T(1,128)S(1)}, u32[]{:S(2)}, u32[]{:S(2)}) %all-to-all-start.3) | async-done | bytes 1179680 | tf_op jit(solution)/shard_map/all_to_all | solution.py:180
  172.5 1.4 slice_multiply_fusion.1
  (160 shorter events, 47.3 us)
Async XLA Ops:
  0.6 2.2 %copy-start.2 = (bf16[64,4,512]{2,1,0:T(4,128)(2,1)S(1)}, bf16[64,4,512]{2,1,0:T(4,128)(2,1)}, u32[]{:S(2)}) copy-start(bf16[64,4,512]{2,1,0:T(4,128)(2,1)} %param.6) | copy-start | bytes 786436
  2.9 8.0 %copy-start.10 = (bf16[3,3,128,128]{3,2,1,0:T(8,128)(2,1)S(1)}, bf16[3,3,128,128]{3,2,1,0:T(8,128)(2,1)}, u32[]{:S(2)}) copy-start(bf16[3,3,128,128]{3,2,1,0:T(8,128)(2,1)} %param.9) | copy-start | bytes 884740
  6.0 9.3 %copy-start.11 = (bf16[128,2,256]{2,1,0:T(2,128)(2,1)S(1)}, bf16[128,2,256]{2,1,0:T(2,128)(2,1)}, u32[]{:S(2)}) copy-start(bf16[128,2,256]{2,1,0:T(2,128)(2,1)} %param.10) | copy-start | bytes 393220
  6.0 31.9 %collective-permute-start.1 = (bf16[128,3,512]{2,0,1:T(8,128)(2,1)}, bf16[128,3,512]{2,0,1:T(8,128)(2,1)}, u32[]{:S(2)}, u32[]{:S(2)}) collective-permute-start(bf16[128,3,512]{2,0,1:T(8,128)(2,1)} %slice.619), channel_id=1, source_target_pairs={{0,2},{2,4},{4,6},{6,8},{8,10},{10,12},{12,14},{14,16},{16,18},{18... | collective-permute-start | bytes 1179656 | tf_op jit(solution)/shard_map/ppermute | solution.py:41
  8.2 30.9 %collective-permute-start.2 = (bf16[128,2,512]{2,0,1:T(8,128)(2,1)}, bf16[128,2,512]{2,0,1:T(8,128)(2,1)}, u32[]{:S(2)}, u32[]{:S(2)}) collective-permute-start(bf16[128,2,512]{2,0,1:T(8,128)(2,1)} %slice.620), channel_id=1, source_target_pairs={{2,0},{4,2},{6,4},{8,6},{10,8},{12,10},{14,12},{16,14},{18,16},{20... | collective-permute-start | bytes 786440 | tf_op jit(solution)/shard_map/ppermute | solution.py:42
  11.8 5.9 %all-to-all-start.1 = ((bf16[2,3,3,128,64]{3,4,2,1,0:T(8,128)(2,1)}), bf16[2,3,3,128,64]{3,4,2,1,0:T(8,128)(2,1)S(1)}, u32[]{:S(2)}, u32[]{:S(2)}) async-start(bf16[2,3,3,128,64]{3,4,2,1,0:T(8,128)(2,1)} %bitcast.398), calls=%async_computation.1 | async-start | bytes 589824 | tf_op jit(solution)/shard_map/all_to_all | solution.py:148
  23.9 4.5 %copy-start.3 = (bf16[3,3,64,128]{3,2,1,0:T(8,128)(2,1)S(1)}, bf16[3,3,64,128]{3,2,1,0:T(8,128)(2,1)}, u32[]{:S(2)}) copy-start(bf16[3,3,64,128]{3,2,1,0:T(8,128)(2,1)} %param.7) | copy-start | bytes 442372
  23.9 4.8 %copy-start.5 = (bf16[3,3,64,128]{3,2,1,0:T(8,128)(2,1)S(1)}, bf16[3,3,64,128]{3,2,1,0:T(8,128)(2,1)}, u32[]{:S(2)}) copy-start(bf16[3,3,64,128]{3,2,1,0:T(8,128)(2,1)} %param.8) | copy-start | bytes 442372
  27.9 9.2 %collective-permute-start = (bf16[64,1,512]{2,0,1:T(8,128)(2,1)}, bf16[64,1,512]{2,0,1:T(8,128)(2,1)}, u32[]{:S(2)}, u32[]{:S(2)}) collective-permute-start(bf16[64,1,512]{2,0,1:T(8,128)(2,1)} %copy.87), channel_id=1, source_target_pairs={{0,254},{2,0},{4,2},{6,4},{8,6},{10,8},{12,10},{14,12},{16,14},{18... | collective-permute-start | bytes 196616 | tf_op jit(solution)/shard_map/ppermute | solution.py:24
  29.8 5.0 %all-to-all-start = ((bf16[2,3,3,128,64]{3,4,2,1,0:T(8,128)(2,1)}), bf16[2,3,3,128,64]{3,4,2,1,0:T(8,128)(2,1)S(1)}, u32[]{:S(2)}, u32[]{:S(2)}) async-start(bf16[2,3,3,128,64]{3,4,2,1,0:T(8,128)(2,1)} %bitcast.399), calls=%async_computation | async-start | bytes 589824 | tf_op jit(solution)/shard_map/all_to_all | solution.py:148
  33.4 1.8 %copy-start = (f32[64,6,514]{0,2,1:T(8,128)S(1)}, f32[64,6,514]{0,2,1:T(8,128)}, u32[]{:S(2)}) copy-start(f32[64,6,514]{0,2,1:T(8,128)} %reshape.65) | copy-start | bytes 2368516
  36.0 0.9 copy-start.1
  39.0 1.1 copy-start.4
  44.2 2.9 %copy-start.6 = (bf16[3,3,64,128]{3,2,1,0:T(8,128)(2,1)S(1)}, bf16[3,3,64,128]{3,2,1,0:T(8,128)(2,1)}, u32[]{:S(2)}) copy-start(bf16[3,3,64,128]{3,2,1,0:T(8,128)(2,1)} %param.8) | copy-start | bytes 442372
  58.5 1.0 copy-start.7
  58.5 1.1 copy-start.8
  58.5 1.2 copy-start.9
  64.3 6.6 %collective-permute-start.3 = (bf16[64,1,512]{2,0,1:T(8,128)(2,1)S(1)}, bf16[64,1,512]{2,0,1:T(8,128)(2,1)S(1)}, u32[]{:S(2)}, u32[]{:S(2)}) collective-permute-start(bf16[64,1,512]{2,0,1:T(8,128)(2,1)S(1)} %get-tuple-element.34), channel_id=1, source_target_pairs={{0,2},{2,4},{4,6},{6,8},{8,10},{10,12},{12,14},{14,16},{16,18},{18... | collective-permute-start | bytes 196616 | tf_op jit(solution)/shard_map/ppermute | solution.py:24
  65.9 5.0 %collective-permute-start.4 = (bf16[64,1,512]{2,0,1:T(8,128)(2,1)S(1)}, bf16[64,1,512]{2,0,1:T(8,128)(2,1)S(1)}, u32[]{:S(2)}, u32[]{:S(2)}) collective-permute-start(bf16[64,1,512]{2,0,1:T(8,128)(2,1)S(1)} %get-tuple-element.35), channel_id=1, source_target_pairs={{0,254},{2,0},{4,2},{6,4},{8,6},{10,8},{12,10},{14,12},{16,14},{18... | collective-permute-start | bytes 196616 | tf_op jit(solution)/shard_map/ppermute | solution.py:24
  76.6 54.5 %all-to-all-start.2 = ((f32[128,1,2304]{2,1,0:T(1,128)}), f32[128,1,2304]{2,1,0:T(1,128)S(1)}, u32[]{:S(2)}, u32[]{:S(2)}) async-start(f32[128,1,2304]{2,1,0:T(1,128)} %bitcast.172), calls=%async_computation.2 | async-start | bytes 2359296 | tf_op jit(solution)/shard_map/all_to_all | solution.py:177
  133.5 39.1 %all-to-all-start.3 = ((f32[128,1,2304]{2,1,0:T(1,128)}), f32[128,1,2304]{2,1,0:T(1,128)S(1)}, u32[]{:S(2)}, u32[]{:S(2)}) async-start(f32[128,1,2304]{2,1,0:T(1,128)} %broadcast_in_dim.2), calls=%async_computation.3 | async-start | bytes 2359296 | tf_op jit(solution)/shard_map/all_to_all | solution.py:180
  142.1 7.4 %collective-permute-start.5 = (bf16[64,1,512]{2,0,1:T(8,128)(2,1)S(1)}, bf16[64,1,512]{2,0,1:T(8,128)(2,1)S(1)}, u32[]{:S(2)}, u32[]{:S(2)}) collective-permute-start(bf16[64,1,512]{2,0,1:T(8,128)(2,1)S(1)} %get-tuple-element.32), channel_id=1, source_target_pairs={{0,2},{2,4},{4,6},{6,8},{8,10},{10,12},{12,14},{14,16},{16,18},{18... | collective-permute-start | bytes 196616 | tf_op jit(solution)/shard_map/ppermute | solution.py:24
  143.6 5.9 %collective-permute-start.6 = (bf16[64,1,512]{2,0,1:T(8,128)(2,1)S(1)}, bf16[64,1,512]{2,0,1:T(8,128)(2,1)S(1)}, u32[]{:S(2)}, u32[]{:S(2)}) collective-permute-start(bf16[64,1,512]{2,0,1:T(8,128)(2,1)S(1)} %get-tuple-element.33), channel_id=1, source_target_pairs={{0,254},{2,0},{4,2},{6,4},{8,6},{10,8},{12,10},{14,12},{16,14},{18... | collective-permute-start | bytes 196616 | tf_op jit(solution)/shard_map/ppermute | solution.py:24

commit v6 on v2

--- a/solution.py
+++ b/solution.py
@@ -34,13 +34,14 @@
 
 
 def widen_by(active, before_rows, after_rows):
-    gathered = lax.all_gather(active, "chan", axis=0, tiled=True)
-    devices, length = lax.axis_size("blk"), gathered.shape[1]
+    devices, length = lax.axis_size("blk"), active.shape[1]
     up = [(i, (i + 1) % devices) for i in range(devices)]
     down = [(j, i) for i, j in up]
-    before = lax.ppermute(gathered[:, length - before_rows :], "blk", up)
-    after = lax.ppermute(gathered[:, :after_rows], "blk", down)
-    return jnp.concatenate([before, gathered, after], axis=1)
+    before = lax.ppermute(active[:, length - before_rows :], "blk", up)
+    after = lax.ppermute(active[:, :after_rows], "blk", down)
+    gathered = lax.all_gather(active, "chan", axis=0, tiled=True)
+    rims = lax.all_gather(jnp.concatenate([before, after], axis=1), "chan", axis=0, tiled=True)
+    return jnp.concatenate([rims[:, :before_rows], gathered, rims[:, before_rows:]], axis=1)
 
 
 def conv_taps(padded, weight):

time: 166 us -> 168 us (1.012)
  local copies, waits for them, and re-layouts: 16.6 us -> 13.7 us
  starting transfers between devices: 41.2 us -> 43.8 us
  blocking collectives: 19.8 us -> 22 us
  other arithmetic: 5.79 us -> 7.83 us
    all_to_all x1, starting transfers between devices: 21.7 us -> 24.3 us  [summed_over_cycle(): pieces = lax.all_to_all(flat.reshape(devices, -1), axis, 0, 0, tiled=True)]
    unnamed x19 -> x16, local copies, waits for them, and re-layouts: 4.46 us -> 6.79 us
    all_gather x0 -> x1, blocking collectives: none -> 2.28 us  [widen_by(): lax.all_gather(jnp.concatenate([before, after], axis=1), 'chan', axis=0,...]
    ppermute x5, starting transfers between devices: 9.04 us -> 11.1 us  [passed_along(): lax.ppermute(shard, axis, [(i, (i + by) % devices) for i in range(devices)])]
    ppermute x2, starting transfers between devices: 4.14 us -> 2.1 us  [the longest x1 1.27 us: widen_by(): before = lax.ppermute(active[:, length - before_rows:], 'blk', up)]
  transfers between devices with their start and end apart: 9 -> 9, of which waited for: 4 -> 4; matrix products, arithmetic and copies ran while one was open for 10% -> 6% of each run, Pallas kernels for 0% -> 0%
where the time goes in v6:
time: 168 us
  waiting for transfers between devices  53.8 us (32%)
  starting transfers between devices  43.8 us (26%)
  matrix products  24.5 us (15%)
  blocking collectives  22 us (13%)
  local copies, waits for them, and re-layouts  13.7 us (8%)
  other arithmetic  7.83 us (5%)
  between operations  2.13 us (1%)
    all_to_all x1, waiting for transfers between devices, summed_over_cycle(): pieces = lax.all_to_all(flat.reshape(devices, -1), axis, 0, 0, tiled=True)  27.3 us
    all_to_all x1, starting transfers between devices, summed_over_cycle(): pieces = lax.all_to_all(flat.reshape(devices, -1), axis, 0, 0, tiled=True)  24.3 us
    all_to_all x1, waiting for transfers between devices, summed_over_cycle(): whole = lax.all_to_all(spread, axis, 0, 0, tiled=True).reshape(-1)  21.4 us
    ppermute x5, starting transfers between devices, passed_along(): lax.ppermute(shard, axis, [(i, (i + by) % devices) for i in range(devices)])  11.1 us
    dot_general x18, matrix products, spread_taps(): jnp.einsum('oi,orw->irw', weight[row_tap, col_tap], framed[:, row_start:r...  7.11 us
    dot_general x18, matrix products, conv_taps(): jnp.einsum('oi,irw->orw', weight[row_tap, col_tap], framed[:, row_tap:row...  6.95 us
    unnamed x16, local copies, waits for them, and re-layouts  6.79 us
    all_to_all x1, starting transfers between devices, summed_over_cycle(): whole = lax.all_to_all(spread, axis, 0, 0, tiled=True).reshape(-1)  6.34 us
  transfers between devices with their start and end apart: 9, of which 4 were waited for; matrix products, arithmetic and copies ran while one was open for 6% of the time, Pallas kernels for 0%

profile of v6, /device:TPU:8, one launch (start us, length us, event | category | flops | bytes accessed | tf_op | source)
XLA Modules:
  0.0 167.8 jit_solution(9603111379449237476)
XLA Ops:
  2.6 2.0 %all_gather.33 = bf16[256,2,256]{0,2,1:T(8,128)(2,1)S(1)} all-gather(bf16[128,2,256]{0,2,1:T(8,128)(2,1)S(1)} %broadcast_select_fusion.2), channel_id=1, replica_groups=mesh['blk'=128,'chan'=2] {'chan'}, dimensions={0}, use_global_device_ids=true | all-gather | bytes 393216 | tf_op jit(solution)/shard_map/all_gather | solution.py:157
  4.8 2.2 %all_gather.32 = bf16[3,3,256,128]{2,3,1,0:T(8,128)(2,1)S(1)} all-gather(bf16[3,3,128,128]{2,3,1,0:T(8,128)(2,1)S(1)} %copy.62), channel_id=1, replica_groups=mesh['blk'=128,'chan'=2] {'chan'}, dimensions={2}, use_global_device_ids=true | all-gather | bytes 884736 | tf_op jit(solution)/shard_map/all_gather | solution.py:146
  12.4 2.6 %collective-permute-start = (bf16[64,1,512]{2,0,1:T(8,128)(2,1)}, bf16[64,1,512]{2,0,1:T(8,128)(2,1)}, u32[]{:S(2)}, u32[]{:S(2)}) collective-permute-start(bf16[64,1,512]{2,0,1:T(8,128)(2,1)} %copy.102), channel_id=1, source_target_pairs={{0,254},{2,0},{4,2},{6,4},{8,6},{10,8},{12,10},{14,12},{16,14},{18... | collective-permute-start | bytes 196616 | tf_op jit(solution)/shard_map/ppermute | solution.py:24
  18.1 1.3 collective-permute-start.1
  20.2 2.2 %all_gather.35 = bf16[128,4,512]{2,0,1:T(8,128)(2,1)S(1)} all-gather(bf16[64,4,512]{2,0,1:T(8,128)(2,1)S(1)} %broadcast_select_fusion.1), channel_id=1, replica_groups=mesh['blk'=128,'chan'=2] {'chan'}, dimensions={0}, use_global_device_ids=true | all-gather | bytes 786432 | tf_op jit(solution)/shard_map/all_gather | solution.py:42
  24.6 2.0 %all_gather.31 = bf16[3,3,128,128]{3,2,1,0:T(8,128)(2,1)S(1)} all-gather(bf16[3,3,64,128]{3,2,1,0:T(8,128)(2,1)S(1)} %copy-done.1), channel_id=1, replica_groups=mesh['blk'=128,'chan'=2] {'chan'}, dimensions={2}, use_global_device_ids=true | all-gather | bytes 442368 | tf_op jit(solution)/shard_map/all_gather | solution.py:146
  28.5 2.3 %all_gather.34 = bf16[128,5,512]{2,0,1:T(8,128)(2,1)S(1)} all-gather(bf16[64,5,512]{2,0,1:T(8,128)(2,1)S(1)} %pad_maximum_fusion.9), channel_id=1, replica_groups=mesh['blk'=128,'chan'=2] {'chan'}, dimensions={0}, use_global_device_ids=true | all-gather | bytes 983040 | tf_op jit(solution)/shard_map/all_gather | solution.py:43
  35.6 2.6 %all_gather.36 = bf16[128,7,512]{2,0,1:T(8,128)(2,1)S(1)} all-gather(bf16[64,7,512]{2,0,1:T(8,128)(2,1)S(1)} %get-tuple-element.37), channel_id=1, replica_groups=mesh['blk'=128,'chan'=2] {'chan'}, dimensions={0}, use_global_device_ids=true | all-gather | bytes 1376256 | tf_op jit(solution)/shard_map/all_gather | solution.py:195
  41.5 2.3 %all_gather.39 = bf16[128,5,512]{2,0,1:T(8,128)(2,1)S(1)} all-gather(bf16[64,5,512]{2,0,1:T(8,128)(2,1)S(1)} %get-tuple-element.43), channel_id=1, replica_groups=mesh['blk'=128,'chan'=2] {'chan'}, dimensions={0}, use_global_device_ids=true | all-gather | bytes 983040 | tf_op jit(solution)/shard_map/all_gather | solution.py:200
  46.2 2.2 %all_gather.37 = bf16[128,4,512]{2,0,1:T(8,128)(2,1)S(1)} all-gather(bf16[64,4,512]{2,0,1:T(8,128)(2,1)S(1)} %fusion.53), channel_id=1, replica_groups=mesh['blk'=128,'chan'=2] {'chan'}, dimensions={0}, use_global_device_ids=true | all-gather | bytes 786432 | tf_op jit(solution)/shard_map/all_gather | solution.py:152
  55.5 4.1 %collective-permute-start.4 = (bf16[64,1,512]{2,0,1:T(8,128)(2,1)S(1)}, bf16[64,1,512]{2,0,1:T(8,128)(2,1)S(1)}, u32[]{:S(2)}, u32[]{:S(2)}) collective-permute-start(bf16[64,1,512]{2,0,1:T(8,128)(2,1)S(1)} %get-tuple-element.33), channel_id=1, source_target_pairs={{0,254},{2,0},{4,2},{6,4},{8,6},{10,8},{12,10},{14,12},{16,14},{18... | collective-permute-start | bytes 196616 | tf_op jit(solution)/shard_map/ppermute | solution.py:24
  59.8 2.0 %collective-permute-done.3 = bf16[64,1,512]{2,0,1:T(8,128)(2,1)S(1)} collective-permute-done((bf16[64,1,512]{2,0,1:T(8,128)(2,1)S(1)}, bf16[64,1,512]{2,0,1:T(8,128)(2,1)S(1)}, u32[]{:S(2)}, u32[]{:S(2)}) %collective-permute-start.3) | collective-permute-done | bytes 65568 | tf_op jit(solution)/shard_map/ppermute | solution.py:24
  66.7 24.3 %all-to-all-start = ((f32[128,1,2304]{2,1,0:T(1,128)}), f32[128,1,2304]{2,1,0:T(1,128)S(1)}, u32[]{:S(2)}, u32[]{:S(2)}) async-start(f32[128,1,2304]{2,1,0:T(1,128)} %bitcast.162), calls=%async_computation | async-start | bytes 2359296 | tf_op jit(solution)/shard_map/all_to_all | solution.py:171
  91.0 2.0 %all_gather.30 = bf16[3,3,128,128]{3,2,1,0:T(8,128)(2,1)S(1)} all-gather(bf16[3,3,64,128]{3,2,1,0:T(8,128)(2,1)S(1)} %copy-done.2), channel_id=1, replica_groups=mesh['blk'=128,'chan'=2] {'chan'}, dimensions={2}, use_global_device_ids=true | all-gather | bytes 442368 | tf_op jit(solution)/shard_map/all_gather | solution.py:146
  93.0 2.2 %all_gather.38 = bf16[128,4,512]{2,0,1:T(8,128)(2,1)S(1)} all-gather(bf16[64,4,512]{2,0,1:T(8,128)(2,1)S(1)} %fusion.60), channel_id=1, replica_groups=mesh['blk'=128,'chan'=2] {'chan'}, dimensions={0}, use_global_device_ids=true | all-gather | bytes 786432 | tf_op jit(solution)/shard_map/all_gather | solution.py:152
  96.4 27.3 %all-to-all-done = f32[128,1,2304]{2,1,0:T(1,128)S(1)} async-done(((f32[128,1,2304]{2,1,0:T(1,128)}), f32[128,1,2304]{2,1,0:T(1,128)S(1)}, u32[]{:S(2)}, u32[]{:S(2)}) %all-to-all-start) | async-done | bytes 1179680 | tf_op jit(solution)/shard_map/all_to_all | solution.py:171
  124.4 1.7 broadcast_in_dim.2
  126.0 6.3 %all-to-all-start.1 = ((f32[128,1,2304]{2,1,0:T(1,128)}), f32[128,1,2304]{2,1,0:T(1,128)S(1)}, u32[]{:S(2)}, u32[]{:S(2)}) async-start(f32[128,1,2304]{2,1,0:T(1,128)} %broadcast_in_dim.2), calls=%async_computation.1 | async-start | bytes 2359296 | tf_op jit(solution)/shard_map/all_to_all | solution.py:174
  134.8 1.5 collective-permute-start.5
  136.4 2.7 %collective-permute-start.6 = (bf16[64,1,512]{2,0,1:T(8,128)(2,1)S(1)}, bf16[64,1,512]{2,0,1:T(8,128)(2,1)S(1)}, u32[]{:S(2)}, u32[]{:S(2)}) collective-permute-start(bf16[64,1,512]{2,0,1:T(8,128)(2,1)S(1)} %get-tuple-element.31), channel_id=1, source_target_pairs={{0,254},{2,0},{4,2},{6,4},{8,6},{10,8},{12,10},{14,12},{16,14},{18... | collective-permute-start | bytes 196616 | tf_op jit(solution)/shard_map/ppermute | solution.py:24
  139.0 3.1 %collective-permute-done.5 = bf16[64,1,512]{2,0,1:T(8,128)(2,1)S(1)} collective-permute-done((bf16[64,1,512]{2,0,1:T(8,128)(2,1)S(1)}, bf16[64,1,512]{2,0,1:T(8,128)(2,1)S(1)}, u32[]{:S(2)}, u32[]{:S(2)}) %collective-permute-start.5) | collective-permute-done | bytes 65568 | tf_op jit(solution)/shard_map/ppermute | solution.py:24
  143.7 21.4 %all-to-all-done.1 = f32[128,1,2304]{2,1,0:T(1,128)S(1)} async-done(((f32[128,1,2304]{2,1,0:T(1,128)}), f32[128,1,2304]{2,1,0:T(1,128)S(1)}, u32[]{:S(2)}, u32[]{:S(2)}) %all-to-all-start.1) | async-done | bytes 1179680 | tf_op jit(solution)/shard_map/all_to_all | solution.py:174
  165.0 1.4 slice_multiply_fusion.1
  166.4 1.3 slice_multiply_fusion
  (138 shorter events, 42.6 us)
Async XLA Ops:
  0.6 3.9 %copy-start.3 = (bf16[3,3,128,128]{3,2,1,0:T(8,128)(2,1)S(1)}, bf16[3,3,128,128]{3,2,1,0:T(8,128)(2,1)}, u32[]{:S(2)}) copy-start(bf16[3,3,128,128]{3,2,1,0:T(8,128)(2,1)} %param.9) | copy-start | bytes 884740
  11.6 4.9 %copy-start = (bf16[64,4,512]{2,1,0:T(4,128)(2,1)S(1)}, bf16[64,4,512]{2,1,0:T(4,128)(2,1)}, u32[]{:S(2)}) copy-start(bf16[64,4,512]{2,1,0:T(4,128)(2,1)} %param.6) | copy-start | bytes 786436
  12.4 14.2 %collective-permute-start = (bf16[64,1,512]{2,0,1:T(8,128)(2,1)}, bf16[64,1,512]{2,0,1:T(8,128)(2,1)}, u32[]{:S(2)}, u32[]{:S(2)}) collective-permute-start(bf16[64,1,512]{2,0,1:T(8,128)(2,1)} %copy.102), channel_id=1, source_target_pairs={{0,254},{2,0},{4,2},{6,4},{8,6},{10,8},{12,10},{14,12},{16,14},{18... | collective-permute-start | bytes 196616 | tf_op jit(solution)/shard_map/ppermute | solution.py:24
  17.3 10.2 %collective-permute-start.2 = (bf16[64,2,512]{2,0,1:T(8,128)(2,1)}, bf16[64,2,512]{2,0,1:T(8,128)(2,1)}, u32[]{:S(2)}, u32[]{:S(2)}) collective-permute-start(bf16[64,2,512]{2,0,1:T(8,128)(2,1)} %slice.578), channel_id=1, source_target_pairs={{2,0},{4,2},{6,4},{8,6},{10,8},{12,10},{14,12},{16,14},{18,16},{20... | collective-permute-start | bytes 393224 | tf_op jit(solution)/shard_map/ppermute | solution.py:41
  18.1 9.4 %collective-permute-start.1 = (bf16[64,3,512]{2,0,1:T(8,128)(2,1)S(1)}, bf16[64,3,512]{2,0,1:T(8,128)(2,1)}, u32[]{:S(2)}, u32[]{:S(2)}) collective-permute-start(bf16[64,3,512]{2,0,1:T(8,128)(2,1)S(1)} %slice.577), channel_id=1, source_target_pairs={{0,2},{2,4},{4,6},{6,8},{8,10},{10,12},{12,14},{14,16},{16,18},{18... | collective-permute-start | bytes 589832 | tf_op jit(solution)/shard_map/ppermute | solution.py:40
  23.7 0.9 copy-start.1
  30.9 0.9 copy-start.2
  55.4 6.5 %collective-permute-start.3 = (bf16[64,1,512]{2,0,1:T(8,128)(2,1)S(1)}, bf16[64,1,512]{2,0,1:T(8,128)(2,1)S(1)}, u32[]{:S(2)}, u32[]{:S(2)}) collective-permute-start(bf16[64,1,512]{2,0,1:T(8,128)(2,1)S(1)} %get-tuple-element.32), channel_id=1, source_target_pairs={{0,2},{2,4},{4,6},{6,8},{8,10},{10,12},{12,14},{14,16},{16,18},{18... | collective-permute-start | bytes 196616 | tf_op jit(solution)/shard_map/ppermute | solution.py:24
  55.5 6.4 %collective-permute-start.4 = (bf16[64,1,512]{2,0,1:T(8,128)(2,1)S(1)}, bf16[64,1,512]{2,0,1:T(8,128)(2,1)S(1)}, u32[]{:S(2)}, u32[]{:S(2)}) collective-permute-start(bf16[64,1,512]{2,0,1:T(8,128)(2,1)S(1)} %get-tuple-element.33), channel_id=1, source_target_pairs={{0,254},{2,0},{4,2},{6,4},{8,6},{10,8},{12,10},{14,12},{16,14},{18... | collective-permute-start | bytes 196616 | tf_op jit(solution)/shard_map/ppermute | solution.py:24
  66.7 57.0 %all-to-all-start = ((f32[128,1,2304]{2,1,0:T(1,128)}), f32[128,1,2304]{2,1,0:T(1,128)S(1)}, u32[]{:S(2)}, u32[]{:S(2)}) async-start(f32[128,1,2304]{2,1,0:T(1,128)} %bitcast.162), calls=%async_computation | async-start | bytes 2359296 | tf_op jit(solution)/shard_map/all_to_all | solution.py:171
  126.0 39.0 %all-to-all-start.1 = ((f32[128,1,2304]{2,1,0:T(1,128)}), f32[128,1,2304]{2,1,0:T(1,128)S(1)}, u32[]{:S(2)}, u32[]{:S(2)}) async-start(f32[128,1,2304]{2,1,0:T(1,128)} %broadcast_in_dim.2), calls=%async_computation.1 | async-start | bytes 2359296 | tf_op jit(solution)/shard_map/all_to_all | solution.py:174
  134.8 7.3 %collective-permute-start.5 = (bf16[64,1,512]{2,0,1:T(8,128)(2,1)S(1)}, bf16[64,1,512]{2,0,1:T(8,128)(2,1)S(1)}, u32[]{:S(2)}, u32[]{:S(2)}) collective-permute-start(bf16[64,1,512]{2,0,1:T(8,128)(2,1)S(1)} %get-tuple-element.30), channel_id=1, source_target_pairs={{0,2},{2,4},{4,6},{6,8},{8,10},{10,12},{12,14},{14,16},{16,18},{18... | collective-permute-start | bytes 196616 | tf_op jit(solution)/shard_map/ppermute | solution.py:24
  136.4 5.8 %collective-permute-start.6 = (bf16[64,1,512]{2,0,1:T(8,128)(2,1)S(1)}, bf16[64,1,512]{2,0,1:T(8,128)(2,1)S(1)}, u32[]{:S(2)}, u32[]{:S(2)}) collective-permute-start(bf16[64,1,512]{2,0,1:T(8,128)(2,1)S(1)} %get-tuple-element.31), channel_id=1, source_target_pairs={{0,254},{2,0},{4,2},{6,4},{8,6},{10,8},{12,10},{14,12},{16,14},{18... | collective-permute-start | bytes 196616 | tf_op jit(solution)/shard_map/ppermute | solution.py:24

commit v7 on v2

--- a/solution.py
+++ b/solution.py
@@ -63,20 +63,15 @@
     row_count = grad_out.shape[1]
     col_count = grad_out.shape[2]
     framed = jnp.pad(padded, ((0, 0), (0, 0), (1, 1)))
-    stacked = []
-    for row_tap in range(3):
-        line = []
-        for col_tap in range(3):
-            line.append(
-                jnp.einsum(
-                    "orw,irw->oi",
-                    grad_out,
-                    framed[:, row_tap : row_tap + row_count, col_tap : col_tap + col_count],
-                    preferred_element_type=jnp.float32,
-                )
-            )
-        stacked.append(jnp.stack(line))
-    return jnp.stack(stacked)
+    views = jnp.stack(
+        [
+            framed[:, row_tap : row_tap + row_count, col_tap : col_tap + col_count]
+            for row_tap in range(3)
+            for col_tap in range(3)
+        ]
+    )
+    taps = jnp.einsum("orw,kirw->koi", grad_out, views, preferred_element_type=jnp.float32)
+    return taps.reshape((3, 3) + taps.shape[1:])
 
 
 def spread_taps(grad_out, weight):

time: 166 us -> 162 us (0.976)
  matrix products: 25.7 us -> 21.5 us
  local copies, waits for them, and re-layouts: 16.6 us -> 19.8 us
  waiting for transfers between devices: 53.8 us -> 51.5 us
  starting transfers between devices: 41.2 us -> 39.1 us
  other arithmetic: 5.79 us -> 7.65 us
    dot_general x18 -> x2, matrix products: 7.29 us -> 3.05 us  [weight_taps(): jnp.einsum('orw,kirw->koi', grad_out, views, preferred_element_type=jnp.f...]
    unnamed x19 -> x32, local copies, waits for them, and re-layouts: 4.46 us -> 7.02 us
    all_to_all x1, starting transfers between devices: 21.7 us -> 19.3 us  [summed_over_cycle(): pieces = lax.all_to_all(flat.reshape(devices, -1), axis, 0, 0, tiled=True)]
    ppermute x5, waiting for transfers between devices: 5.13 us -> 2.98 us  [passed_along(): lax.ppermute(shard, axis, [(i, (i + by) % devices) for i in range(devices)])]
  transfers between devices with their start and end apart: 9 -> 9, of which waited for: 4 -> 3; matrix products, arithmetic and copies ran while one was open for 10% -> 13% of each run, Pallas kernels for 0% -> 0%
where the time goes in v7:
time: 162 us; the launch traced here: 161 us
  waiting for transfers between devices  51.5 us (32%)
  starting transfers between devices  39.1 us (24%)
  matrix products  21.5 us (13%)
  local copies, waits for them, and re-layouts  19.8 us (12%)
  blocking collectives  19.8 us (12%)
  other arithmetic  7.65 us (5%)
  between operations  2.11 us (1%)
    all_to_all x1, waiting for transfers between devices, summed_over_cycle(): pieces = lax.all_to_all(flat.reshape(devices, -1), axis, 0, 0, tiled=True)  27.3 us
    all_to_all x1, waiting for transfers between devices, summed_over_cycle(): whole = lax.all_to_all(spread, axis, 0, 0, tiled=True).reshape(-1)  21.2 us
    all_to_all x1, starting transfers between devices, summed_over_cycle(): pieces = lax.all_to_all(flat.reshape(devices, -1), axis, 0, 0, tiled=True)  19.3 us
    ppermute x5, starting transfers between devices, passed_along(): lax.ppermute(shard, axis, [(i, (i + by) % devices) for i in range(devices)])  9.3 us
    dot_general x18, matrix products, conv_taps(): jnp.einsum('oi,irw->orw', weight[row_tap, col_tap], framed[:, row_tap:row...  7.17 us
    dot_general x18, matrix products, spread_taps(): jnp.einsum('oi,orw->irw', weight[row_tap, col_tap], framed[:, row_start:r...  7.11 us
    unnamed x32, local copies, waits for them, and re-layouts  7.02 us
    all_to_all x1, starting transfers between devices, summed_over_cycle(): whole = lax.all_to_all(spread, axis, 0, 0, tiled=True).reshape(-1)  6.34 us
  transfers between devices with their start and end apart: 9, of which 3 were waited for; matrix products, arithmetic and copies ran while one was open for 13% of the time, Pallas kernels for 0%

profile of v7, /device:TPU:8, one launch (start us, length us, event | category | flops | bytes accessed | tf_op | source)
XLA Modules:
  0.0 161.4 jit_solution(18438336296300883969)
XLA Ops:
  3.9 2.3 %all_gather.31 = bf16[128,4,512]{2,0,1:T(8,128)(2,1)S(1)} all-gather(bf16[64,4,512]{2,0,1:T(8,128)(2,1)S(1)} %broadcast_select_fusion.1), channel_id=1, replica_groups=mesh['blk'=128,'chan'=2] {'chan'}, dimensions={0}, use_global_device_ids=true | all-gather | bytes 786432 | tf_op jit(solution)/shard_map/all_gather | solution.py:37
  7.0 1.5 collective-permute-start.1
  9.2 2.6 %collective-permute-start.2 = (bf16[128,2,512]{2,0,1:T(8,128)(2,1)}, bf16[128,2,512]{2,0,1:T(8,128)(2,1)}, u32[]{:S(2)}, u32[]{:S(2)}) collective-permute-start(bf16[128,2,512]{2,0,1:T(8,128)(2,1)} %slice.570), channel_id=1, source_target_pairs={{2,0},{4,2},{6,4},{8,6},{10,8},{12,10},{14,12},{16,14},{18,16},{20... | collective-permute-start | bytes 786440 | tf_op jit(solution)/shard_map/ppermute | solution.py:42
  12.2 2.0 %all_gather.30 = bf16[256,2,256]{0,2,1:T(8,128)(2,1)S(1)} all-gather(bf16[128,2,256]{0,2,1:T(8,128)(2,1)S(1)} %broadcast_select_fusion.2), channel_id=1, replica_groups=mesh['blk'=128,'chan'=2] {'chan'}, dimensions={0}, use_global_device_ids=true | all-gather | bytes 393216 | tf_op jit(solution)/shard_map/all_gather | solution.py:151
  14.4 2.2 %all_gather.29 = bf16[3,3,256,128]{2,3,1,0:T(8,128)(2,1)S(1)} all-gather(bf16[3,3,128,128]{2,3,1,0:T(8,128)(2,1)S(1)} %copy.62), channel_id=1, replica_groups=mesh['blk'=128,'chan'=2] {'chan'}, dimensions={2}, use_global_device_ids=true | all-gather | bytes 884736 | tf_op jit(solution)/shard_map/all_gather | solution.py:140
  20.1 2.3 %reshape.51 = f32[64,6,514]{0,2,1:T(8,128)} reshape(f32[64,3,2,257,2]{0,4,3,2,1:T(2,128)S(1)} %copy.65) | data formatting | bytes 1579008 | tf_op jit(solution)/shard_map/reshape | solution.py:122
  27.2 2.0 %all_gather.28 = bf16[3,3,128,128]{3,2,1,0:T(8,128)(2,1)S(1)} all-gather(bf16[3,3,64,128]{3,2,1,0:T(8,128)(2,1)S(1)} %copy-done), channel_id=1, replica_groups=mesh['blk'=128,'chan'=2] {'chan'}, dimensions={2}, use_global_device_ids=true | all-gather | bytes 442368 | tf_op jit(solution)/shard_map/all_gather | solution.py:140
  35.5 2.6 %all_gather.32 = bf16[128,7,512]{2,0,1:T(8,128)(2,1)S(1)} all-gather(bf16[64,7,512]{2,0,1:T(8,128)(2,1)S(1)} %get-tuple-element.41), channel_id=1, replica_groups=mesh['blk'=128,'chan'=2] {'chan'}, dimensions={0}, use_global_device_ids=true | all-gather | bytes 1376256 | tf_op jit(solution)/shard_map/all_gather | solution.py:189
  41.5 2.3 %all_gather.35 = bf16[128,5,512]{2,0,1:T(8,128)(2,1)S(1)} all-gather(bf16[64,5,512]{2,0,1:T(8,128)(2,1)S(1)} %get-tuple-element.47), channel_id=1, replica_groups=mesh['blk'=128,'chan'=2] {'chan'}, dimensions={0}, use_global_device_ids=true | all-gather | bytes 983040 | tf_op jit(solution)/shard_map/all_gather | solution.py:194
  47.6 2.2 %all_gather.33 = bf16[128,4,512]{2,0,1:T(8,128)(2,1)S(1)} all-gather(bf16[64,4,512]{2,0,1:T(8,128)(2,1)S(1)} %fusion.63), channel_id=1, replica_groups=mesh['blk'=128,'chan'=2] {'chan'}, dimensions={0}, use_global_device_ids=true | all-gather | bytes 786432 | tf_op jit(solution)/shard_map/all_gather | solution.py:146
  53.4 1.6 collective-permute-start.3
  55.0 2.6 %collective-permute-start.4 = (bf16[64,1,512]{2,0,1:T(8,128)(2,1)S(1)}, bf16[64,1,512]{2,0,1:T(8,128)(2,1)S(1)}, u32[]{:S(2)}, u32[]{:S(2)}) collective-permute-start(bf16[64,1,512]{2,0,1:T(8,128)(2,1)S(1)} %get-tuple-element.35), channel_id=1, source_target_pairs={{0,254},{2,0},{4,2},{6,4},{8,6},{10,8},{12,10},{14,12},{16,14},{18... | collective-permute-start | bytes 196616 | tf_op jit(solution)/shard_map/ppermute | solution.py:24
  59.4 1.5 fusion.103
  62.7 1.5 fusion.105
  65.4 19.3 %all-to-all-start = ((f32[128,1,2304]{2,1,0:T(1,128)}), f32[128,1,2304]{2,1,0:T(1,128)S(1)}, u32[]{:S(2)}, u32[]{:S(2)}) async-start(f32[128,1,2304]{2,1,0:T(1,128)} %bitcast.146), calls=%async_computation | async-start | bytes 2359296 | tf_op jit(solution)/shard_map/all_to_all | solution.py:165
  84.7 2.0 %all_gather.27 = bf16[3,3,128,128]{3,2,1,0:T(8,128)(2,1)S(1)} all-gather(bf16[3,3,64,128]{3,2,1,0:T(8,128)(2,1)S(1)} %copy-done.1), channel_id=1, replica_groups=mesh['blk'=128,'chan'=2] {'chan'}, dimensions={2}, use_global_device_ids=true | all-gather | bytes 442368 | tf_op jit(solution)/shard_map/all_gather | solution.py:140
  86.7 2.2 %all_gather.34 = bf16[128,4,512]{2,0,1:T(8,128)(2,1)S(1)} all-gather(bf16[64,4,512]{2,0,1:T(8,128)(2,1)S(1)} %fusion.70), channel_id=1, replica_groups=mesh['blk'=128,'chan'=2] {'chan'}, dimensions={0}, use_global_device_ids=true | all-gather | bytes 786432 | tf_op jit(solution)/shard_map/all_gather | solution.py:146
  90.1 27.3 %all-to-all-done = f32[128,1,2304]{2,1,0:T(1,128)S(1)} async-done(((f32[128,1,2304]{2,1,0:T(1,128)}), f32[128,1,2304]{2,1,0:T(1,128)S(1)}, u32[]{:S(2)}, u32[]{:S(2)}) %all-to-all-start) | async-done | bytes 1179680 | tf_op jit(solution)/shard_map/all_to_all | solution.py:165
  118.1 1.7 %broadcast_in_dim.2 = f32[128,1,2304]{2,1,0:T(1,128)} broadcast(f32[2304]{0:T(1024)S(1)} %reduce_sum.9), dimensions={2} | broadcast | bytes 1188864 | tf_op jit(solution)/shard_map/broadcast_in_dim | solution.py:167
  119.7 6.3 %all-to-all-start.1 = ((f32[128,1,2304]{2,1,0:T(1,128)}), f32[128,1,2304]{2,1,0:T(1,128)S(1)}, u32[]{:S(2)}, u32[]{:S(2)}) async-start(f32[128,1,2304]{2,1,0:T(1,128)} %broadcast_in_dim.2), calls=%async_computation.1 | async-start | bytes 2359296 | tf_op jit(solution)/shard_map/all_to_all | solution.py:168
  128.5 1.8 %collective-permute-start.5 = (bf16[64,1,512]{2,0,1:T(8,128)(2,1)S(1)}, bf16[64,1,512]{2,0,1:T(8,128)(2,1)S(1)}, u32[]{:S(2)}, u32[]{:S(2)}) collective-permute-start(bf16[64,1,512]{2,0,1:T(8,128)(2,1)S(1)} %get-tuple-element.32), channel_id=1, source_target_pairs={{0,2},{2,4},{4,6},{6,8},{8,10},{10,12},{12,14},{14,16},{16,18},{18... | collective-permute-start | bytes 196616 | tf_op jit(solution)/shard_map/ppermute | solution.py:24
  130.3 2.7 %collective-permute-start.6 = (bf16[64,1,512]{2,0,1:T(8,128)(2,1)S(1)}, bf16[64,1,512]{2,0,1:T(8,128)(2,1)S(1)}, u32[]{:S(2)}, u32[]{:S(2)}) collective-permute-start(bf16[64,1,512]{2,0,1:T(8,128)(2,1)S(1)} %get-tuple-element.33), channel_id=1, source_target_pairs={{0,254},{2,0},{4,2},{6,4},{8,6},{10,8},{12,10},{14,12},{16,14},{18... | collective-permute-start | bytes 196616 | tf_op jit(solution)/shard_map/ppermute | solution.py:24
  133.0 3.0 %collective-permute-done.5 = bf16[64,1,512]{2,0,1:T(8,128)(2,1)S(1)} collective-permute-done((bf16[64,1,512]{2,0,1:T(8,128)(2,1)S(1)}, bf16[64,1,512]{2,0,1:T(8,128)(2,1)S(1)}, u32[]{:S(2)}, u32[]{:S(2)}) %collective-permute-start.5) | collective-permute-done | bytes 65568 | tf_op jit(solution)/shard_map/ppermute | solution.py:24
  137.5 21.2 %all-to-all-done.1 = f32[128,1,2304]{2,1,0:T(1,128)S(1)} async-done(((f32[128,1,2304]{2,1,0:T(1,128)}), f32[128,1,2304]{2,1,0:T(1,128)S(1)}, u32[]{:S(2)}, u32[]{:S(2)}) %all-to-all-start.1) | async-done | bytes 1179680 | tf_op jit(solution)/shard_map/all_to_all | solution.py:168
  (130 shorter events, 42.6 us)
Async XLA Ops:
  2.8 9.0 %copy-start.3 = (bf16[128,2,256]{2,1,0:T(2,128)(2,1)S(1)}, bf16[128,2,256]{2,1,0:T(2,128)(2,1)}, u32[]{:S(2)}) copy-start(bf16[128,2,256]{2,1,0:T(2,128)(2,1)} %param.10) | copy-start | bytes 393220
  3.9 10.3 %copy-start.2 = (bf16[3,3,128,128]{3,2,1,0:T(8,128)(2,1)S(1)}, bf16[3,3,128,128]{3,2,1,0:T(8,128)(2,1)}, u32[]{:S(2)}) copy-start(bf16[3,3,128,128]{3,2,1,0:T(8,128)(2,1)} %param.9) | copy-start | bytes 884740
  7.0 22.3 %collective-permute-start.1 = (bf16[128,3,512]{2,0,1:T(8,128)(2,1)}, bf16[128,3,512]{2,0,1:T(8,128)(2,1)}, u32[]{:S(2)}, u32[]{:S(2)}) collective-permute-start(bf16[128,3,512]{2,0,1:T(8,128)(2,1)} %slice.569), channel_id=1, source_target_pairs={{0,2},{2,4},{4,6},{6,8},{8,10},{10,12},{12,14},{14,16},{16,18},{18... | collective-permute-start | bytes 1179656 | tf_op jit(solution)/shard_map/ppermute | solution.py:41
  9.2 21.3 %collective-permute-start.2 = (bf16[128,2,512]{2,0,1:T(8,128)(2,1)}, bf16[128,2,512]{2,0,1:T(8,128)(2,1)}, u32[]{:S(2)}, u32[]{:S(2)}) collective-permute-start(bf16[128,2,512]{2,0,1:T(8,128)(2,1)} %slice.570), channel_id=1, source_target_pairs={{2,0},{4,2},{6,4},{8,6},{10,8},{12,10},{14,12},{16,14},{18,16},{20... | collective-permute-start | bytes 786440 | tf_op jit(solution)/shard_map/ppermute | solution.py:42
  23.5 5.7 %collective-permute-start = (bf16[64,1,512]{2,0,1:T(8,128)(2,1)S(1)}, bf16[64,1,512]{2,0,1:T(8,128)(2,1)S(1)}, u32[]{:S(2)}, u32[]{:S(2)}) collective-permute-start(bf16[64,1,512]{2,0,1:T(8,128)(2,1)S(1)} %copy.104), channel_id=1, source_target_pairs={{0,254},{2,0},{4,2},{6,4},{8,6},{10,8},{12,10},{14,12},{16,14},{18... | collective-permute-start | bytes 196616 | tf_op jit(solution)/shard_map/ppermute | solution.py:24
  26.3 0.9 copy-start
  30.3 1.2 copy-start.1
  53.4 8.8 %collective-permute-start.3 = (bf16[64,1,512]{2,0,1:T(8,128)(2,1)S(1)}, bf16[64,1,512]{2,0,1:T(8,128)(2,1)S(1)}, u32[]{:S(2)}, u32[]{:S(2)}) collective-permute-start(bf16[64,1,512]{2,0,1:T(8,128)(2,1)S(1)} %get-tuple-element.34), channel_id=1, source_target_pairs={{0,2},{2,4},{4,6},{6,8},{8,10},{10,12},{12,14},{14,16},{16,18},{18... | collective-permute-start | bytes 196616 | tf_op jit(solution)/shard_map/ppermute | solution.py:24
  55.0 7.3 %collective-permute-start.4 = (bf16[64,1,512]{2,0,1:T(8,128)(2,1)S(1)}, bf16[64,1,512]{2,0,1:T(8,128)(2,1)S(1)}, u32[]{:S(2)}, u32[]{:S(2)}) collective-permute-start(bf16[64,1,512]{2,0,1:T(8,128)(2,1)S(1)} %get-tuple-element.35), channel_id=1, source_target_pairs={{0,254},{2,0},{4,2},{6,4},{8,6},{10,8},{12,10},{14,12},{16,14},{18... | collective-permute-start | bytes 196616 | tf_op jit(solution)/shard_map/ppermute | solution.py:24
  65.4 52.0 %all-to-all-start = ((f32[128,1,2304]{2,1,0:T(1,128)}), f32[128,1,2304]{2,1,0:T(1,128)S(1)}, u32[]{:S(2)}, u32[]{:S(2)}) async-start(f32[128,1,2304]{2,1,0:T(1,128)} %bitcast.146), calls=%async_computation | async-start | bytes 2359296 | tf_op jit(solution)/shard_map/all_to_all | solution.py:165
  119.7 39.0 %all-to-all-start.1 = ((f32[128,1,2304]{2,1,0:T(1,128)}), f32[128,1,2304]{2,1,0:T(1,128)S(1)}, u32[]{:S(2)}, u32[]{:S(2)}) async-start(f32[128,1,2304]{2,1,0:T(1,128)} %broadcast_in_dim.2), calls=%async_computation.1 | async-start | bytes 2359296 | tf_op jit(solution)/shard_map/all_to_all | solution.py:168
  128.5 7.5 %collective-permute-start.5 = (bf16[64,1,512]{2,0,1:T(8,128)(2,1)S(1)}, bf16[64,1,512]{2,0,1:T(8,128)(2,1)S(1)}, u32[]{:S(2)}, u32[]{:S(2)}) collective-permute-start(bf16[64,1,512]{2,0,1:T(8,128)(2,1)S(1)} %get-tuple-element.32), channel_id=1, source_target_pairs={{0,2},{2,4},{4,6},{6,8},{8,10},{10,12},{12,14},{14,16},{16,18},{18... | collective-permute-start | bytes 196616 | tf_op jit(solution)/shard_map/ppermute | solution.py:24
  130.3 5.7 %collective-permute-start.6 = (bf16[64,1,512]{2,0,1:T(8,128)(2,1)S(1)}, bf16[64,1,512]{2,0,1:T(8,128)(2,1)S(1)}, u32[]{:S(2)}, u32[]{:S(2)}) collective-permute-start(bf16[64,1,512]{2,0,1:T(8,128)(2,1)S(1)} %get-tuple-element.33), channel_id=1, source_target_pairs={{0,254},{2,0},{4,2},{6,4},{8,6},{10,8},{12,10},{14,12},{16,14},{18... | collective-permute-start | bytes 196616 | tf_op jit(solution)/shard_map/ppermute | solution.py:24
